TPU v7x, 512 devices: a whole 4x8x8 slice. The times are simulated.
512 devices in a mesh: sec: 4 (over z_lo), gx: 8 (over z_hi, x), gy: 16 (over y, core).
Axes of the slice: x: 4, y: 8, z: 8 (z_hi: 2, z_lo: 4; z = z_hi * 4 + z_lo), core: 2. Of those that a mesh axis runs over, the one named last changes fastest.
Arguments:
- soil_class: int32 [256, 4096], P('gx', 'gy'), may hold values from 0 to 11
- geology_class: int32 [256, 4096], P('gx', 'gy'), may hold values from 0 to 15
- land_mask: int32 [256, 4096], P('gx', 'gy'), may hold values 0 or 1
- river_mask: int32 [256, 4096], P('gx', 'gy'), may hold values 0 or 1
- elevation: float32 [256, 4096], P('gx', 'gy'), may hold values from -6 to 6
- roughness: float32 [256, 4096], P('gx', 'gy'), may hold values from 0.02 to 0.11
- rainfall: float32 [256, 4096], P('gx', 'gy'), may hold values from 0.05 to 1
- potential_evap: float32 [256, 4096], P('gx', 'gy'), may hold values from 0.05 to 0.5
- surface_head: float32 [256, 4096], P('gx', 'gy'), may hold values from -3 to 3
- pressure: float32 [8, 256, 4096], P('sec', 'gx', 'gy'), may hold values from -6 to 6
- storage: float32 [8, 256, 4096], P('sec', 'gx', 'gy'), may hold values from 0.2 to 2
- soil_embed: bfloat16 [12, 128], replicated, may hold values from -4 to 4
- geology_embed: bfloat16 [16, 128], replicated, may hold values from -4 to 4
- conv_weight: bfloat16 [3, 3, 128, 128], replicated, may hold values from -0.1875 to 0.1875
- out_weight: bfloat16 [128, 8], replicated, may hold values from -0.5 to 0.5
Outputs:
- pressure_out: float32 [8, 256, 4096], P('sec', 'gx', 'gy')
- head_out: float32 [256, 4096], P('gx', 'gy')
All inputs are finite; a program needn't handle non-finite values. No bound on the sum of `land_mask` or of `river_mask` on one device may be relied on, other than what follows from the above.
Results may differ from a plain program's by a relative error of at most 0.0041.
Values sent between devices are 32-bit elements; how exact they have to be, the bound alone decides.
No kernel may reach another device: no remote copies, remote signals or barrier semaphores. Data moves between devices by JAX's collectives and lax.ppermute only.
A program may use at most 64 MiB of HBM per device.

v0:
```python
import jax
import jax.numpy as jnp
from jax import lax
from jax.sharding import PartitionSpec as P

SWEEPS = 4
CYCLES = 4
infil_rate = 0.3
lateral = 1.0
vertical = 0.5


def padded(block, sides, width):
    for axis, dim in sides:
        count = lax.axis_size(axis)
        forward = [(i, i + 1) for i in range(count - 1)]
        backward = [(target, source) for source, target in forward]
        low = lax.ppermute(
            lax.slice_in_dim(block, block.shape[dim] - width, None, axis=dim), axis, forward
        )
        high = lax.ppermute(lax.slice_in_dim(block, 0, width, axis=dim), axis, backward)
        block = jnp.concatenate([low, block, high], axis=dim)
    return block


def spread(value, axis, root):
    mine = lax.axis_index(axis) == root
    return lax.psum(jnp.where(mine, value, jnp.zeros_like(value)), axis)


def infiltration(land_frac, top_cond, surface, top_press):
    return land_frac * (infil_rate * top_cond / (1.0 + top_cond)) * (surface - top_press)


def evaporation_loss(land_frac, potential, top_press):
    return land_frac * potential * jax.nn.sigmoid(top_press)


def surface_flux(level_pad, rough_pad):
    centre_level = level_pad[1:-1, 1:-1]
    centre_rough = rough_pad[1:-1, 1:-1]
    total = jnp.zeros_like(centre_level)
    pairs = (
        (level_pad[2:, 1:-1], rough_pad[2:, 1:-1]),
        (level_pad[:-2, 1:-1], rough_pad[:-2, 1:-1]),
        (level_pad[1:-1, 2:], rough_pad[1:-1, 2:]),
        (level_pad[1:-1, :-2], rough_pad[1:-1, :-2]),
    )
    for near_level, near_rough in pairs:
        total = total + 0.5 * (centre_rough + near_rough) * (near_level - centre_level)
    return total


def shifted(values):
    return [
        (values[:-2, 1:-1, 1:-1], vertical),
        (values[2:, 1:-1, 1:-1], vertical),
        (values[1:-1, :-2, 1:-1], lateral),
        (values[1:-1, 2:, 1:-1], lateral),
        (values[1:-1, 1:-1, 2:], lateral),
        (values[1:-1, 1:-1, :-2], lateral),
    ]


def jacobi_sweep(press_pad, cond_pad, rhs_mid, store_mid):
    cond_mid = cond_pad[1:-1, 1:-1, 1:-1]
    diagonal = store_mid
    total = rhs_mid
    for (near_press, factor), (near_cond, unused) in zip(shifted(press_pad), shifted(cond_pad)):
        face = factor * 0.5 * (cond_mid + near_cond)
        diagonal = diagonal + face
        total = total + face * near_press
    return total / diagonal


def tile_features(soil_class, geology_class, soil_embed, geology_embed):
    soil_onehot = (
        soil_class[:, :, None] == jnp.arange(soil_embed.shape[0], dtype=jnp.int32)
    ).astype(jnp.bfloat16)
    geology_onehot = (
        geology_class[:, :, None] == jnp.arange(geology_embed.shape[0], dtype=jnp.int32)
    ).astype(jnp.bfloat16)
    total = jnp.einsum("xys,sc->xyc", soil_onehot, soil_embed, preferred_element_type=jnp.float32)
    total = total + jnp.einsum(
        "xys,sc->xyc", geology_onehot, geology_embed, preferred_element_type=jnp.float32
    )
    return total.astype(jnp.bfloat16)


def conv_relu(features_pad, kernel):
    convolved = lax.conv_general_dilated(
        features_pad[None],
        kernel,
        (1, 1),
        "VALID",
        dimension_numbers=("NHWC", "HWIO", "NCHW"),
        preferred_element_type=jnp.float32,
    )[0]
    return jax.nn.relu(convolved).astype(jnp.bfloat16)


def shards(
    soil_class,
    geology_class,
    land_mask,
    river_mask,
    elevation,
    roughness,
    rainfall,
    potential_evap,
    surface_head,
    pressure,
    storage,
    soil_embed,
    geology_embed,
    conv_weight,
    out_weight,
):
    sec_count = lax.axis_size("sec")
    sec_index = lax.axis_index("sec")
    layers_dev, tile_rows, tile_cols = pressure.shape
    class_pad = (
        padded(jnp.stack((soil_class + 1, geology_class + 1)), (("gx", 1), ("gy", 2)), 1) - 1
    )
    features_pad = tile_features(class_pad[0], class_pad[1], soil_embed, geology_embed)
    hidden = conv_relu(features_pad, conv_weight)
    own_out = lax.dynamic_slice_in_dim(out_weight, sec_index * layers_dev, layers_dev, 1)
    logits = jnp.einsum("cxy,cl->lxy", hidden, own_out, preferred_element_type=jnp.float32)
    conduct = jnp.exp(logits)
    depth = 1
    coeff_pad = padded(jnp.stack((conduct, storage)), (("sec", 1), ("gx", 2), ("gy", 3)), depth)
    cond_pad = coeff_pad[0]
    top_cond = spread(conduct[0], "sec", 0)
    land_frac = land_mask.astype(jnp.float32)
    river_frac = river_mask.astype(jnp.float32)
    rough = land_frac * (1.0 + river_frac) * roughness
    rough_pad = padded(rough, (("gx", 0), ("gy", 1)), 1)
    strip_rows = tile_rows // sec_count
    first_row = sec_index * strip_rows

    def strip_of(values):
        return lax.dynamic_slice_in_dim(values, first_row, strip_rows, 0)

    strip_land = strip_of(land_frac)
    strip_rain = strip_of(rainfall)
    strip_potential = strip_of(potential_evap)
    strip_cond = strip_of(top_cond)
    strip_rough = lax.dynamic_slice_in_dim(rough_pad, first_row, strip_rows + 2, 0)
    layer_ids = sec_index * layers_dev + jnp.arange(layers_dev, dtype=jnp.int32)
    top_layer = (layer_ids == 0).astype(jnp.float32)[:, None, None]
    surface = surface_head
    press = pressure
    for cycle in range(CYCLES):
        top_press = spread(press[0], "sec", 0)
        level_pad = padded(surface + elevation, (("gx", 0), ("gy", 1)), 1)
        level_strip = lax.dynamic_slice_in_dim(level_pad, first_row, strip_rows + 2, 0)
        flux = surface_flux(level_strip, strip_rough)
        old_strip = strip_of(surface)
        top_strip = strip_of(top_press)
        infil = infiltration(strip_land, strip_cond, old_strip, top_strip)
        evap = evaporation_loss(strip_land, strip_potential, top_strip)
        new_strip = old_strip + strip_land * (strip_rain - infil + flux)
        source_strip = infil - evap
        surface, source = (
            lax.all_gather(new_strip, "sec", axis=0, tiled=True),
            lax.all_gather(source_strip, "sec", axis=0, tiled=True),
        )
        rhs = storage * press + top_layer * source[None]
        for sweep in range(SWEEPS):
            press_pad = padded(press, (("sec", 0), ("gx", 1), ("gy", 2)), 1)
            press = jacobi_sweep(press_pad, cond_pad, rhs, storage)
    return (press, surface)


def solution(mesh):
    in_specs = (
        P("gx", "gy"),
        P("gx", "gy"),
        P("gx", "gy"),
        P("gx", "gy"),
        P("gx", "gy"),
        P("gx", "gy"),
        P("gx", "gy"),
        P("gx", "gy"),
        P("gx", "gy"),
        P("sec", "gx", "gy"),
        P("sec", "gx", "gy"),
        P(),
        P(),
        P(),
        P(),
    )
    out_specs = (P("sec", "gx", "gy"), P("gx", "gy"))
    return jax.shard_map(shards, mesh=mesh, in_specs=in_specs, out_specs=out_specs, check_vma=False)
```

profile of v0, /device:TPU:38, one launch (start us, length us, event | category | flops | bytes accessed | tf_op | source)
XLA Modules:
  0.0 819.4 jit_solution(7540490617223454841)
XLA Ops:
  8.0 10.8 %collective-permute-start = (s32[2,1,256]{2,1,0:T(1,128)S(1)}, s32[2,1,256]{2,1,0:T(1,128)S(1)}, u32[]{:S(2)}, u32[]{:S(2)}) collective-permute-start(s32[2,1,256]{2,1,0:T(1,128)S(1)} %get-tuple-element.138), channel_id=1, source_target_pairs={{0,16},{16,32},{32,48},{48,64},{64,80},{80,96},{96,112},{1,17},{17... | collective-permute-start | bytes 6152 | tf_op jit(solution)/shard_map/ppermute | solution.py:18
  21.6 9.9 %collective-permute-start.38 = (f32[1,256]{1,0:T(1,128)S(1)}, f32[1,256]{1,0:T(1,128)S(1)}, u32[]{:S(2)}, u32[]{:S(2)}) collective-permute-start(f32[1,256]{1,0:T(1,128)S(1)} %get-tuple-element.161), channel_id=1, source_target_pairs={{0,16},{16,32},{32,48},{48,64},{64,80},{80,96},{96,112},{1,17},{17... | collective-permute-start | bytes 3080 | tf_op jit(solution)/shard_map/ppermute | solution.py:18
  34.3 9.9 %collective-permute-start.34 = (f32[1,256]{1,0:T(1,128)S(1)}, f32[1,256]{1,0:T(1,128)S(1)}, u32[]{:S(2)}, u32[]{:S(2)}) collective-permute-start(f32[1,256]{1,0:T(1,128)S(1)} %get-tuple-element.159), channel_id=1, source_target_pairs={{0,16},{16,32},{32,48},{48,64},{64,80},{80,96},{96,112},{1,17},{17... | collective-permute-start | bytes 3080 | tf_op jit(solution)/shard_map/ppermute | solution.py:18
  53.8 4.1 collective-permute-done.35
  70.2 4.9 collective-permute-start.3
  86.2 5.4 maximum_convert_fusion
  98.5 8.8 %collective-permute-start.12 = (f32[4,1,256]{2,1,0:T(1,128)S(1)}, f32[4,1,256]{2,1,0:T(1,128)S(1)}, u32[]{:S(2)}, u32[]{:S(2)}) collective-permute-start(f32[4,1,256]{2,1,0:T(1,128)S(1)} %get-tuple-element.91), channel_id=1, source_target_pairs={{0,16},{16,32},{32,48},{48,64},{64,80},{80,96},{96,112},{1,17},{17... | collective-permute-start | bytes 12296 | tf_op jit(solution)/shard_map/ppermute | solution.py:18
  109.2 4.5 collective-permute-start.4
  124.3 6.8 collective-permute-start.6
  133.1 38.9 %all-reduce.3.cloned.1.call-done = (f32[32,256]{1,0:T(8,128)}, f32[32,256]{1,0:T(8,128)}) async-done(((f32[32,256]{1,0:T(8,128)}, f32[32,256]{1,0:T(8,128)}), (f32[32,256]{1,0:T(8,128)}, f32[32,256]{1,0:T(8,128)})) %all-reduce.3.cloned.1.call-update) | async-done | bytes 65552 | tf_op jit(solution)/shard_map/psum | solution.py:28
  175.7 4.9 collective-permute-start.9
  180.6 13.1 %all_gather.24 = f32[32,256]{1,0:T(8,128)S(1)} all-gather(f32[8,256]{1,0:T(8,128)S(1)} %get-tuple-element.21), channel_id=1, replica_groups=mesh['sec'=4,'gx'=8,'gy'=16] {'sec'}, dimensions={0}, use_global_device_ids=true | all-gather | bytes 40960 | tf_op jit(solution)/shard_map/all_gather | solution.py:166
  197.0 4.2 collective-permute-done.17
  201.3 6.9 collective-permute-start.18
  210.1 9.6 %collective-permute-done.19 = f32[4,1,256]{2,1,0:T(1,128)S(1)} collective-permute-done((f32[4,1,256]{2,1,0:T(1,128)S(1)}, f32[4,1,256]{2,1,0:T(1,128)S(1)}, u32[]{:S(2)}, u32[]{:S(2)}) %collective-permute-start.19) | collective-permute-done | bytes 4128 | tf_op jit(solution)/shard_map/ppermute | solution.py:21
  224.1 4.5 collective-permute-done.21
  233.2 4.3 collective-permute-done.23
  243.4 13.1 %all_gather.25 = f32[32,256]{1,0:T(8,128)S(1)} all-gather(f32[8,256]{1,0:T(8,128)S(1)} %get-tuple-element.8), channel_id=1, replica_groups=mesh['sec'=4,'gx'=8,'gy'=16] {'sec'}, dimensions={0}, use_global_device_ids=true | all-gather | bytes 40960 | tf_op jit(solution)/shard_map/all_gather | solution.py:165
  261.0 7.9 collective-permute-start.66
  274.7 5.8 collective-permute-done.67
  280.5 8.6 %collective-permute-start.30 = (f32[4,1,256]{2,1,0:T(1,128)S(1)}, f32[4,1,256]{2,1,0:T(1,128)S(1)}, u32[]{:S(2)}, u32[]{:S(2)}) collective-permute-start(f32[4,1,256]{2,1,0:T(1,128)S(1)} %get-tuple-element.83), channel_id=1, source_target_pairs={{0,16},{16,32},{32,48},{48,64},{64,80},{80,96},{96,112},{1,17},{17... | collective-permute-start | bytes 12296 | tf_op jit(solution)/shard_map/ppermute | solution.py:18
  293.1 4.9 collective-permute-start.69
  305.3 4.4 collective-permute-done.33
  314.0 19.2 %psum.37 = f32[32,256]{1,0:T(8,128)S(1)} all-reduce(f32[32,256]{1,0:T(8,128)S(1)} %get-tuple-element.127), channel_id=1, replica_groups=mesh['sec'=4,'gx'=8,'gy'=16] {'sec'}, use_global_device_ids=true, to_apply=%region_2.3 | all-reduce | flops 8192 | bytes 65536 | tf_op jit(solution)/shard_map/psum | solution.py:28
  333.2 7.2 collective-permute-start.44
  342.5 9.5 %collective-permute-done.45 = f32[4,1,256]{2,1,0:T(1,128)S(1)} collective-permute-done((f32[4,1,256]{2,1,0:T(1,128)S(1)}, f32[4,1,256]{2,1,0:T(1,128)S(1)}, u32[]{:S(2)}, u32[]{:S(2)}) %collective-permute-start.45) | collective-permute-done | bytes 4128 | tf_op jit(solution)/shard_map/ppermute | solution.py:21
  356.4 13.2 %all_gather.26 = f32[32,256]{1,0:T(8,128)S(1)} all-gather(f32[8,256]{1,0:T(8,128)S(1)} %get-tuple-element.102), channel_id=1, replica_groups=mesh['sec'=4,'gx'=8,'gy'=16] {'sec'}, dimensions={0}, use_global_device_ids=true | all-gather | bytes 40960 | tf_op jit(solution)/shard_map/all_gather | solution.py:166
  372.6 4.2 collective-permute-done.49
  382.7 7.6 collective-permute-done.51
  394.8 4.5 collective-permute-done.53
  404.7 4.2 collective-permute-done.55
  414.8 13.1 %all_gather.27 = f32[32,256]{1,0:T(8,128)S(1)} all-gather(f32[8,256]{1,0:T(8,128)S(1)} %get-tuple-element.101), channel_id=1, replica_groups=mesh['sec'=4,'gx'=8,'gy'=16] {'sec'}, dimensions={0}, use_global_device_ids=true | all-gather | bytes 40960 | tf_op jit(solution)/shard_map/all_gather | solution.py:165
  432.4 7.9 collective-permute-start.94
  445.1 6.8 collective-permute-done.95
  451.9 7.6 collective-permute-start.62
  463.5 4.9 collective-permute-start.97
  475.7 4.4 collective-permute-done.65
  485.2 18.3 %psum.38 = f32[32,256]{1,0:T(8,128)S(1)} all-reduce(f32[32,256]{1,0:T(8,128)S(1)} %get-tuple-element.118), channel_id=1, replica_groups=mesh['sec'=4,'gx'=8,'gy'=16] {'sec'}, use_global_device_ids=true, to_apply=%region_3.4 | all-reduce | flops 8192 | bytes 65536 | tf_op jit(solution)/shard_map/psum | solution.py:28
  503.6 7.2 collective-permute-start.72
  512.8 9.5 %collective-permute-done.73 = f32[4,1,256]{2,1,0:T(1,128)S(1)} collective-permute-done((f32[4,1,256]{2,1,0:T(1,128)S(1)}, f32[4,1,256]{2,1,0:T(1,128)S(1)}, u32[]{:S(2)}, u32[]{:S(2)}) %collective-permute-start.73) | collective-permute-done | bytes 4128 | tf_op jit(solution)/shard_map/ppermute | solution.py:21
  526.8 13.2 %all_gather.28 = f32[32,256]{1,0:T(8,128)S(1)} all-gather(f32[8,256]{1,0:T(8,128)S(1)} %get-tuple-element.100), channel_id=1, replica_groups=mesh['sec'=4,'gx'=8,'gy'=16] {'sec'}, dimensions={0}, use_global_device_ids=true | all-gather | bytes 40960 | tf_op jit(solution)/shard_map/all_gather | solution.py:166
  543.0 4.2 collective-permute-done.77
  553.1 7.6 collective-permute-done.79
  565.1 4.5 collective-permute-done.81
  575.1 4.2 collective-permute-done.83
  585.2 13.1 %all_gather.29 = f32[32,256]{1,0:T(8,128)S(1)} all-gather(f32[8,256]{1,0:T(8,128)S(1)} %get-tuple-element.99), channel_id=1, replica_groups=mesh['sec'=4,'gx'=8,'gy'=16] {'sec'}, dimensions={0}, use_global_device_ids=true | all-gather | bytes 40960 | tf_op jit(solution)/shard_map/all_gather | solution.py:165
  602.8 7.9 collective-permute-start.122
  615.5 6.8 collective-permute-done.123
  622.3 7.6 collective-permute-start.90
  633.8 4.9 collective-permute-start.125
  646.0 4.4 collective-permute-done.93
  655.6 18.3 %psum.39 = f32[32,256]{1,0:T(8,128)S(1)} all-reduce(f32[32,256]{1,0:T(8,128)S(1)} %get-tuple-element.109), channel_id=1, replica_groups=mesh['sec'=4,'gx'=8,'gy'=16] {'sec'}, use_global_device_ids=true, to_apply=%region_4.5 | all-reduce | flops 8192 | bytes 65536 | tf_op jit(solution)/shard_map/psum | solution.py:28
  673.9 7.2 collective-permute-start.100
  683.2 9.5 %collective-permute-done.101 = f32[4,1,256]{2,1,0:T(1,128)S(1)} collective-permute-done((f32[4,1,256]{2,1,0:T(1,128)S(1)}, f32[4,1,256]{2,1,0:T(1,128)S(1)}, u32[]{:S(2)}, u32[]{:S(2)}) %collective-permute-start.101) | collective-permute-done | bytes 4128 | tf_op jit(solution)/shard_map/ppermute | solution.py:21
  697.2 13.2 %all_gather.30 = f32[32,256]{1,0:T(8,128)S(1)} all-gather(f32[8,256]{1,0:T(8,128)S(1)} %get-tuple-element.98), channel_id=1, replica_groups=mesh['sec'=4,'gx'=8,'gy'=16] {'sec'}, dimensions={0}, use_global_device_ids=true | all-gather | bytes 40960 | tf_op jit(solution)/shard_map/all_gather | solution.py:166
  713.4 4.2 collective-permute-done.105
  723.5 7.6 collective-permute-done.107
  735.5 4.5 collective-permute-done.109
  745.5 4.2 collective-permute-done.111
  755.6 7.6 collective-permute-done.113
  767.6 4.5 collective-permute-done.115
  775.8 4.2 collective-permute-done.117
  785.9 7.6 collective-permute-done.119
  797.9 13.2 %all_gather.31 = f32[32,256]{1,0:T(8,128)S(1)} all-gather(f32[8,256]{1,0:T(8,128)S(1)} %get-tuple-element.97), channel_id=1, replica_groups=mesh['sec'=4,'gx'=8,'gy'=16] {'sec'}, dimensions={0}, use_global_device_ids=true | all-gather | bytes 40960 | tf_op jit(solution)/shard_map/all_gather | solution.py:165
  (358 shorter events, 272.9 us)
Async XLA Ops:
  7.2 164.8 %all-reduce.3.cloned.1.call-start = ((), (), s32[]{:S(2)}) async-start(), calls=%async_computation | async-start | bytes 131072 | tf_op jit(solution)/shard_map/psum | solution.py:28
  8.0 56.0 %collective-permute-start = (s32[2,1,256]{2,1,0:T(1,128)S(1)}, s32[2,1,256]{2,1,0:T(1,128)S(1)}, u32[]{:S(2)}, u32[]{:S(2)}) collective-permute-start(s32[2,1,256]{2,1,0:T(1,128)S(1)} %get-tuple-element.138), channel_id=1, source_target_pairs={{0,16},{16,32},{32,48},{48,64},{64,80},{80,96},{96,112},{1,17},{17... | collective-permute-start | bytes 6152 | tf_op jit(solution)/shard_map/ppermute | solution.py:18
  18.9 49.3 %collective-permute-start.1 = (s32[2,1,256]{2,1,0:T(1,128)S(1)}, s32[2,1,256]{2,1,0:T(1,128)S(1)}, u32[]{:S(2)}, u32[]{:S(2)}) collective-permute-start(s32[2,1,256]{2,1,0:T(1,128)S(1)} %get-tuple-element.139), channel_id=1, source_target_pairs={{16,0},{32,16},{48,32},{64,48},{80,64},{96,80},{112,96},{17,1},{33... | collective-permute-start | bytes 6152 | tf_op jit(solution)/shard_map/ppermute | solution.py:21
  21.6 24.8 %collective-permute-start.38 = (f32[1,256]{1,0:T(1,128)S(1)}, f32[1,256]{1,0:T(1,128)S(1)}, u32[]{:S(2)}, u32[]{:S(2)}) collective-permute-start(f32[1,256]{1,0:T(1,128)S(1)} %get-tuple-element.161), channel_id=1, source_target_pairs={{0,16},{16,32},{32,48},{48,64},{64,80},{80,96},{96,112},{1,17},{17... | collective-permute-start | bytes 3080 | tf_op jit(solution)/shard_map/ppermute | solution.py:18
  31.6 16.8 %collective-permute-start.39 = (f32[1,256]{1,0:T(1,128)S(1)}, f32[1,256]{1,0:T(1,128)S(1)}, u32[]{:S(2)}, u32[]{:S(2)}) collective-permute-start(f32[1,256]{1,0:T(1,128)S(1)} %get-tuple-element.162), channel_id=1, source_target_pairs={{16,0},{32,16},{48,32},{64,48},{80,64},{96,80},{112,96},{17,1},{33... | collective-permute-start | bytes 3080 | tf_op jit(solution)/shard_map/ppermute | solution.py:21
  34.3 17.5 %collective-permute-start.34 = (f32[1,256]{1,0:T(1,128)S(1)}, f32[1,256]{1,0:T(1,128)S(1)}, u32[]{:S(2)}, u32[]{:S(2)}) collective-permute-start(f32[1,256]{1,0:T(1,128)S(1)} %get-tuple-element.159), channel_id=1, source_target_pairs={{0,16},{16,32},{32,48},{48,64},{64,80},{80,96},{96,112},{1,17},{17... | collective-permute-start | bytes 3080 | tf_op jit(solution)/shard_map/ppermute | solution.py:18
  48.3 50.1 %collective-permute-start.10 = (f32[1,32,256]{2,1,0:T(8,128)S(1)}, f32[1,32,256]{2,1,0:T(8,128)S(1)}, u32[]{:S(2)}, u32[]{:S(2)}) collective-permute-start(f32[1,32,256]{2,1,0:T(8,128)S(1)} %get-tuple-element.141), channel_id=1, source_target_pairs={{0,128},{128,256},{256,384},{1,129},{129,257},{257,385},{2,130},{1... | collective-permute-start | bytes 98312 | tf_op jit(solution)/shard_map/ppermute | solution.py:18
  59.9 38.6 %collective-permute-start.11 = (f32[1,32,256]{2,1,0:T(8,128)S(1)}, f32[1,32,256]{2,1,0:T(8,128)S(1)}, u32[]{:S(2)}, u32[]{:S(2)}) collective-permute-start(f32[1,32,256]{2,1,0:T(8,128)S(1)} %get-tuple-element.142), channel_id=1, source_target_pairs={{128,0},{256,128},{384,256},{129,1},{257,129},{385,257},{130,2},{2... | collective-permute-start | bytes 98312 | tf_op jit(solution)/shard_map/ppermute | solution.py:21
  98.5 16.6 %collective-permute-start.12 = (f32[4,1,256]{2,1,0:T(1,128)S(1)}, f32[4,1,256]{2,1,0:T(1,128)S(1)}, u32[]{:S(2)}, u32[]{:S(2)}) collective-permute-start(f32[4,1,256]{2,1,0:T(1,128)S(1)} %get-tuple-element.91), channel_id=1, source_target_pairs={{0,16},{16,32},{32,48},{48,64},{64,80},{80,96},{96,112},{1,17},{17... | collective-permute-start | bytes 12296 | tf_op jit(solution)/shard_map/ppermute | solution.py:18
  107.3 11.5 %collective-permute-start.13 = (f32[4,1,256]{2,1,0:T(1,128)S(1)}, f32[4,1,256]{2,1,0:T(1,128)S(1)}, u32[]{:S(2)}, u32[]{:S(2)}) collective-permute-start(f32[4,1,256]{2,1,0:T(1,128)S(1)} %get-tuple-element.92), channel_id=1, source_target_pairs={{16,0},{32,16},{48,32},{64,48},{80,64},{96,80},{112,96},{17,1},{33... | collective-permute-start | bytes 12296 | tf_op jit(solution)/shard_map/ppermute | solution.py:21
  109.2 15.1 %collective-permute-start.4 = (f32[2,1,32,256]{3,2,1,0:T(8,128)S(1)}, f32[2,1,32,256]{3,2,1,0:T(8,128)S(1)}, u32[]{:S(2)}, u32[]{:S(2)}) collective-permute-start(f32[2,1,32,256]{3,2,1,0:T(8,128)S(1)} %get-tuple-element.89), channel_id=1, source_target_pairs={{0,128},{128,256},{256,384},{1,129},{129,257},{257,385},{2,130},{1... | collective-permute-start | bytes 196616 | tf_op jit(solution)/shard_map/ppermute | solution.py:18
  118.9 75.0 %collective-permute-start.14 = (f32[4,34,1]{2,1,0:T(8,128)S(1)}, f32[4,34,1]{2,1,0:T(8,128)S(1)}, u32[]{:S(2)}, u32[]{:S(2)}) collective-permute-start(f32[4,34,1]{2,1,0:T(8,128)S(1)} %get-tuple-element.57), channel_id=1, source_target_pairs={{1,0},{2,1},{3,2},{4,3},{5,4},{6,5},{7,6},{8,7},{9,8},{10,9},{11,1... | collective-permute-start | bytes 1640 | tf_op jit(solution)/shard_map/ppermute | solution.py:21
  122.4 71.5 %collective-permute-start.15 = (f32[4,34,1]{2,1,0:T(8,128)S(1)}, f32[4,34,1]{2,1,0:T(8,128)S(1)}, u32[]{:S(2)}, u32[]{:S(2)}) collective-permute-start(f32[4,34,1]{2,1,0:T(8,128)S(1)} %get-tuple-element.58), channel_id=1, source_target_pairs={{0,1},{1,2},{2,3},{3,4},{4,5},{5,6},{6,7},{7,8},{8,9},{9,10},{10,1... | collective-permute-start | bytes 1640 | tf_op jit(solution)/shard_map/ppermute | solution.py:18
  124.3 49.2 %collective-permute-start.6 = (f32[2,4,1,256]{3,2,1,0:T(1,128)S(1)}, f32[2,4,1,256]{3,2,1,0:T(1,128)S(1)}, u32[]{:S(2)}, u32[]{:S(2)}) collective-permute-start(f32[2,4,1,256]{3,2,1,0:T(1,128)S(1)} %get-tuple-element.25), channel_id=1, source_target_pairs={{0,16},{16,32},{32,48},{48,64},{64,80},{80,96},{96,112},{1,17},{17... | collective-permute-start | bytes 24584 | tf_op jit(solution)/shard_map/ppermute | solution.py:18
  131.2 42.4 %collective-permute-start.7 = (f32[2,4,1,256]{3,2,1,0:T(1,128)S(1)}, f32[2,4,1,256]{3,2,1,0:T(1,128)S(1)}, u32[]{:S(2)}, u32[]{:S(2)}) collective-permute-start(f32[2,4,1,256]{3,2,1,0:T(1,128)S(1)} %get-tuple-element.26), channel_id=1, source_target_pairs={{16,0},{32,16},{48,32},{64,48},{80,64},{96,80},{112,96},{17,1},{33... | collective-permute-start | bytes 24584 | tf_op jit(solution)/shard_map/ppermute | solution.py:21
  173.8 19.9 %collective-permute-start.8 = (f32[2,4,34,1]{3,2,1,0:T(8,128)S(1)}, f32[2,4,34,1]{3,2,1,0:T(8,128)S(1)}, u32[]{:S(2)}, u32[]{:S(2)}) collective-permute-start(f32[2,4,34,1]{3,2,1,0:T(8,128)S(1)} %get-tuple-element.23), channel_id=1, source_target_pairs={{0,1},{1,2},{2,3},{3,4},{4,5},{5,6},{6,7},{7,8},{8,9},{9,10},{10,1... | collective-permute-start | bytes 3272 | tf_op jit(solution)/shard_map/ppermute | solution.py:18
  175.7 18.0 %collective-permute-start.9 = (f32[2,4,34,1]{3,2,1,0:T(8,128)S(1)}, f32[2,4,34,1]{3,2,1,0:T(8,128)S(1)}, u32[]{:S(2)}, u32[]{:S(2)}) collective-permute-start(f32[2,4,34,1]{3,2,1,0:T(8,128)S(1)} %get-tuple-element.24), channel_id=1, source_target_pairs={{1,0},{2,1},{3,2},{4,3},{5,4},{6,5},{7,6},{8,7},{9,8},{10,9},{11,1... | collective-permute-start | bytes 3272 | tf_op jit(solution)/shard_map/ppermute | solution.py:21
  237.5 19.0 %collective-permute-start.24 = (f32[4,1,256]{2,1,0:T(1,128)S(1)}, f32[4,1,256]{2,1,0:T(1,128)S(1)}, u32[]{:S(2)}, u32[]{:S(2)}) collective-permute-start(f32[4,1,256]{2,1,0:T(1,128)S(1)} %get-tuple-element.85), channel_id=1, source_target_pairs={{0,16},{16,32},{32,48},{48,64},{64,80},{80,96},{96,112},{1,17},{17... | collective-permute-start | bytes 12296 | tf_op jit(solution)/shard_map/ppermute | solution.py:18
  239.4 17.1 %collective-permute-start.25 = (f32[4,1,256]{2,1,0:T(1,128)S(1)}, f32[4,1,256]{2,1,0:T(1,128)S(1)}, u32[]{:S(2)}, u32[]{:S(2)}) collective-permute-start(f32[4,1,256]{2,1,0:T(1,128)S(1)} %get-tuple-element.86), channel_id=1, source_target_pairs={{16,0},{32,16},{48,32},{64,48},{80,64},{96,80},{112,96},{17,1},{33... | collective-permute-start | bytes 12296 | tf_op jit(solution)/shard_map/ppermute | solution.py:21
  256.7 14.4 %collective-permute-start.26 = (f32[4,34,1]{2,1,0:T(8,128)S(1)}, f32[4,34,1]{2,1,0:T(8,128)S(1)}, u32[]{:S(2)}, u32[]{:S(2)}) collective-permute-start(f32[4,34,1]{2,1,0:T(8,128)S(1)} %get-tuple-element.53), channel_id=1, source_target_pairs={{1,0},{2,1},{3,2},{4,3},{5,4},{6,5},{7,6},{8,7},{9,8},{10,9},{11,1... | collective-permute-start | bytes 1640 | tf_op jit(solution)/shard_map/ppermute | solution.py:21
  258.6 12.5 %collective-permute-start.27 = (f32[4,34,1]{2,1,0:T(8,128)S(1)}, f32[4,34,1]{2,1,0:T(8,128)S(1)}, u32[]{:S(2)}, u32[]{:S(2)}) collective-permute-start(f32[4,34,1]{2,1,0:T(8,128)S(1)} %get-tuple-element.54), channel_id=1, source_target_pairs={{0,1},{1,2},{2,3},{3,4},{4,5},{5,6},{6,7},{7,8},{8,9},{9,10},{10,1... | collective-permute-start | bytes 1640 | tf_op jit(solution)/shard_map/ppermute | solution.py:18
  261.0 13.7 %collective-permute-start.66 = (f32[1,256]{1,0:T(1,128)S(1)}, f32[1,256]{1,0:T(1,128)S(1)}, u32[]{:S(2)}, u32[]{:S(2)}) collective-permute-start(f32[1,256]{1,0:T(1,128)S(1)} %get-tuple-element.157), channel_id=1, source_target_pairs={{0,16},{16,32},{32,48},{48,64},{64,80},{80,96},{96,112},{1,17},{17... | collective-permute-start | bytes 3080 | tf_op jit(solution)/shard_map/ppermute | solution.py:18
  280.5 17.4 %collective-permute-start.30 = (f32[4,1,256]{2,1,0:T(1,128)S(1)}, f32[4,1,256]{2,1,0:T(1,128)S(1)}, u32[]{:S(2)}, u32[]{:S(2)}) collective-permute-start(f32[4,1,256]{2,1,0:T(1,128)S(1)} %get-tuple-element.83), channel_id=1, source_target_pairs={{0,16},{16,32},{32,48},{48,64},{64,80},{80,96},{96,112},{1,17},{17... | collective-permute-start | bytes 12296 | tf_op jit(solution)/shard_map/ppermute | solution.py:18
  289.1 11.5 %collective-permute-start.31 = (f32[4,1,256]{2,1,0:T(1,128)S(1)}, f32[4,1,256]{2,1,0:T(1,128)S(1)}, u32[]{:S(2)}, u32[]{:S(2)}) collective-permute-start(f32[4,1,256]{2,1,0:T(1,128)S(1)} %get-tuple-element.84), channel_id=1, source_target_pairs={{16,0},{32,16},{48,32},{64,48},{80,64},{96,80},{112,96},{17,1},{33... | collective-permute-start | bytes 12296 | tf_op jit(solution)/shard_map/ppermute | solution.py:21
  291.1 14.0 %collective-permute-start.68 = (f32[34,1]{1,0:T(8,128)S(1)}, f32[34,1]{1,0:T(8,128)S(1)}, u32[]{:S(2)}, u32[]{:S(2)}) collective-permute-start(f32[34,1]{1,0:T(8,128)S(1)} %get-tuple-element.148), channel_id=1, source_target_pairs={{0,1},{1,2},{2,3},{3,4},{4,5},{5,6},{6,7},{7,8},{8,9},{9,10},{10,1... | collective-permute-start | bytes 416 | tf_op jit(solution)/shard_map/ppermute | solution.py:18
  293.1 12.1 %collective-permute-start.69 = (f32[34,1]{1,0:T(8,128)S(1)}, f32[34,1]{1,0:T(8,128)S(1)}, u32[]{:S(2)}, u32[]{:S(2)}) collective-permute-start(f32[34,1]{1,0:T(8,128)S(1)} %get-tuple-element.147), channel_id=1, source_target_pairs={{1,0},{2,1},{3,2},{4,3},{5,4},{6,5},{7,6},{8,7},{9,8},{10,9},{11,1... | collective-permute-start | bytes 416 | tf_op jit(solution)/shard_map/ppermute | solution.py:21
  309.8 23.4 %collective-permute-start.42 = (f32[1,32,256]{2,1,0:T(8,128)S(1)}, f32[1,32,256]{2,1,0:T(8,128)S(1)}, u32[]{:S(2)}, u32[]{:S(2)}) collective-permute-start(f32[1,32,256]{2,1,0:T(8,128)S(1)} %get-tuple-element.128), channel_id=1, source_target_pairs={{0,128},{128,256},{256,384},{1,129},{129,257},{257,385},{2,130},{1... | collective-permute-start | bytes 98312 | tf_op jit(solution)/shard_map/ppermute | solution.py:18
  312.7 20.5 %collective-permute-start.43 = (f32[1,32,256]{2,1,0:T(8,128)S(1)}, f32[1,32,256]{2,1,0:T(8,128)S(1)}, u32[]{:S(2)}, u32[]{:S(2)}) collective-permute-start(f32[1,32,256]{2,1,0:T(8,128)S(1)} %get-tuple-element.129), channel_id=1, source_target_pairs={{128,0},{256,128},{384,256},{129,1},{257,129},{385,257},{130,2},{2... | collective-permute-start | bytes 98312 | tf_op jit(solution)/shard_map/ppermute | solution.py:21
  340.4 11.5 %collective-permute-start.45 = (f32[4,1,256]{2,1,0:T(1,128)S(1)}, f32[4,1,256]{2,1,0:T(1,128)S(1)}, u32[]{:S(2)}, u32[]{:S(2)}) collective-permute-start(f32[4,1,256]{2,1,0:T(1,128)S(1)} %get-tuple-element.82), channel_id=1, source_target_pairs={{16,0},{32,16},{48,32},{64,48},{80,64},{96,80},{112,96},{17,1},{33... | collective-permute-start | bytes 12296 | tf_op jit(solution)/shard_map/ppermute | solution.py:21
  352.1 17.5 %collective-permute-start.46 = (f32[4,34,1]{2,1,0:T(8,128)S(1)}, f32[4,34,1]{2,1,0:T(8,128)S(1)}, u32[]{:S(2)}, u32[]{:S(2)}) collective-permute-start(f32[4,34,1]{2,1,0:T(8,128)S(1)} %get-tuple-element.49), channel_id=1, source_target_pairs={{1,0},{2,1},{3,2},{4,3},{5,4},{6,5},{7,6},{8,7},{9,8},{10,9},{11,1... | collective-permute-start | bytes 1640 | tf_op jit(solution)/shard_map/ppermute | solution.py:21
  354.0 15.6 %collective-permute-start.47 = (f32[4,34,1]{2,1,0:T(8,128)S(1)}, f32[4,34,1]{2,1,0:T(8,128)S(1)}, u32[]{:S(2)}, u32[]{:S(2)}) collective-permute-start(f32[4,34,1]{2,1,0:T(8,128)S(1)} %get-tuple-element.50), channel_id=1, source_target_pairs={{0,1},{1,2},{2,3},{3,4},{4,5},{5,6},{6,7},{7,8},{8,9},{9,10},{10,1... | collective-permute-start | bytes 1640 | tf_op jit(solution)/shard_map/ppermute | solution.py:18
  378.8 11.5 %collective-permute-start.51 = (f32[4,1,256]{2,1,0:T(1,128)S(1)}, f32[4,1,256]{2,1,0:T(1,128)S(1)}, u32[]{:S(2)}, u32[]{:S(2)}) collective-permute-start(f32[4,1,256]{2,1,0:T(1,128)S(1)} %get-tuple-element.80), channel_id=1, source_target_pairs={{16,0},{32,16},{48,32},{64,48},{80,64},{96,80},{112,96},{17,1},{33... | collective-permute-start | bytes 12296 | tf_op jit(solution)/shard_map/ppermute | solution.py:21
  408.9 19.0 %collective-permute-start.56 = (f32[4,1,256]{2,1,0:T(1,128)S(1)}, f32[4,1,256]{2,1,0:T(1,128)S(1)}, u32[]{:S(2)}, u32[]{:S(2)}) collective-permute-start(f32[4,1,256]{2,1,0:T(1,128)S(1)} %get-tuple-element.77), channel_id=1, source_target_pairs={{0,16},{16,32},{32,48},{48,64},{64,80},{80,96},{96,112},{1,17},{17... | collective-permute-start | bytes 12296 | tf_op jit(solution)/shard_map/ppermute | solution.py:18
  410.9 17.1 %collective-permute-start.57 = (f32[4,1,256]{2,1,0:T(1,128)S(1)}, f32[4,1,256]{2,1,0:T(1,128)S(1)}, u32[]{:S(2)}, u32[]{:S(2)}) collective-permute-start(f32[4,1,256]{2,1,0:T(1,128)S(1)} %get-tuple-element.78), channel_id=1, source_target_pairs={{16,0},{32,16},{48,32},{64,48},{80,64},{96,80},{112,96},{17,1},{33... | collective-permute-start | bytes 12296 | tf_op jit(solution)/shard_map/ppermute | solution.py:21
  428.1 14.2 %collective-permute-start.58 = (f32[4,34,1]{2,1,0:T(8,128)S(1)}, f32[4,34,1]{2,1,0:T(8,128)S(1)}, u32[]{:S(2)}, u32[]{:S(2)}) collective-permute-start(f32[4,34,1]{2,1,0:T(8,128)S(1)} %get-tuple-element.45), channel_id=1, source_target_pairs={{1,0},{2,1},{3,2},{4,3},{5,4},{6,5},{7,6},{8,7},{9,8},{10,9},{11,1... | collective-permute-start | bytes 1640 | tf_op jit(solution)/shard_map/ppermute | solution.py:21
  430.0 12.3 %collective-permute-start.59 = (f32[4,34,1]{2,1,0:T(8,128)S(1)}, f32[4,34,1]{2,1,0:T(8,128)S(1)}, u32[]{:S(2)}, u32[]{:S(2)}) collective-permute-start(f32[4,34,1]{2,1,0:T(8,128)S(1)} %get-tuple-element.46), channel_id=1, source_target_pairs={{0,1},{1,2},{2,3},{3,4},{4,5},{5,6},{6,7},{7,8},{8,9},{9,10},{10,1... | collective-permute-start | bytes 1640 | tf_op jit(solution)/shard_map/ppermute | solution.py:18
  432.4 12.6 %collective-permute-start.94 = (f32[1,256]{1,0:T(1,128)S(1)}, f32[1,256]{1,0:T(1,128)S(1)}, u32[]{:S(2)}, u32[]{:S(2)}) collective-permute-start(f32[1,256]{1,0:T(1,128)S(1)} %get-tuple-element.155), channel_id=1, source_target_pairs={{0,16},{16,32},{32,48},{48,64},{64,80},{80,96},{96,112},{1,17},{17... | collective-permute-start | bytes 3080 | tf_op jit(solution)/shard_map/ppermute | solution.py:18
  451.9 16.4 %collective-permute-start.62 = (f32[4,1,256]{2,1,0:T(1,128)S(1)}, f32[4,1,256]{2,1,0:T(1,128)S(1)}, u32[]{:S(2)}, u32[]{:S(2)}) collective-permute-start(f32[4,1,256]{2,1,0:T(1,128)S(1)} %get-tuple-element.75), channel_id=1, source_target_pairs={{0,16},{16,32},{32,48},{48,64},{64,80},{80,96},{96,112},{1,17},{17... | collective-permute-start | bytes 12296 | tf_op jit(solution)/shard_map/ppermute | solution.py:18
  459.5 11.5 %collective-permute-start.63 = (f32[4,1,256]{2,1,0:T(1,128)S(1)}, f32[4,1,256]{2,1,0:T(1,128)S(1)}, u32[]{:S(2)}, u32[]{:S(2)}) collective-permute-start(f32[4,1,256]{2,1,0:T(1,128)S(1)} %get-tuple-element.76), channel_id=1, source_target_pairs={{16,0},{32,16},{48,32},{64,48},{80,64},{96,80},{112,96},{17,1},{33... | collective-permute-start | bytes 12296 | tf_op jit(solution)/shard_map/ppermute | solution.py:21
  461.6 14.0 %collective-permute-start.96 = (f32[34,1]{1,0:T(8,128)S(1)}, f32[34,1]{1,0:T(8,128)S(1)}, u32[]{:S(2)}, u32[]{:S(2)}) collective-permute-start(f32[34,1]{1,0:T(8,128)S(1)} %get-tuple-element.146), channel_id=1, source_target_pairs={{0,1},{1,2},{2,3},{3,4},{4,5},{5,6},{6,7},{7,8},{8,9},{9,10},{10,1... | collective-permute-start | bytes 416 | tf_op jit(solution)/shard_map/ppermute | solution.py:18
  463.5 12.1 %collective-permute-start.97 = (f32[34,1]{1,0:T(8,128)S(1)}, f32[34,1]{1,0:T(8,128)S(1)}, u32[]{:S(2)}, u32[]{:S(2)}) collective-permute-start(f32[34,1]{1,0:T(8,128)S(1)} %get-tuple-element.145), channel_id=1, source_target_pairs={{1,0},{2,1},{3,2},{4,3},{5,4},{6,5},{7,6},{8,7},{9,8},{10,9},{11,1... | collective-permute-start | bytes 416 | tf_op jit(solution)/shard_map/ppermute | solution.py:21
  480.2 23.3 %collective-permute-start.70 = (f32[1,32,256]{2,1,0:T(8,128)S(1)}, f32[1,32,256]{2,1,0:T(8,128)S(1)}, u32[]{:S(2)}, u32[]{:S(2)}) collective-permute-start(f32[1,32,256]{2,1,0:T(8,128)S(1)} %get-tuple-element.119), channel_id=1, source_target_pairs={{0,128},{128,256},{256,384},{1,129},{129,257},{257,385},{2,130},{1... | collective-permute-start | bytes 98312 | tf_op jit(solution)/shard_map/ppermute | solution.py:18
  483.9 19.6 %collective-permute-start.71 = (f32[1,32,256]{2,1,0:T(8,128)S(1)}, f32[1,32,256]{2,1,0:T(8,128)S(1)}, u32[]{:S(2)}, u32[]{:S(2)}) collective-permute-start(f32[1,32,256]{2,1,0:T(8,128)S(1)} %get-tuple-element.120), channel_id=1, source_target_pairs={{128,0},{256,128},{384,256},{129,1},{257,129},{385,257},{130,2},{2... | collective-permute-start | bytes 98312 | tf_op jit(solution)/shard_map/ppermute | solution.py:21
  522.4 17.5 %collective-permute-start.74 = (f32[4,34,1]{2,1,0:T(8,128)S(1)}, f32[4,34,1]{2,1,0:T(8,128)S(1)}, u32[]{:S(2)}, u32[]{:S(2)}) collective-permute-start(f32[4,34,1]{2,1,0:T(8,128)S(1)} %get-tuple-element.41), channel_id=1, source_target_pairs={{1,0},{2,1},{3,2},{4,3},{5,4},{6,5},{7,6},{8,7},{9,8},{10,9},{11,1... | collective-permute-start | bytes 1640 | tf_op jit(solution)/shard_map/ppermute | solution.py:21
  524.4 15.6 %collective-permute-start.75 = (f32[4,34,1]{2,1,0:T(8,128)S(1)}, f32[4,34,1]{2,1,0:T(8,128)S(1)}, u32[]{:S(2)}, u32[]{:S(2)}) collective-permute-start(f32[4,34,1]{2,1,0:T(8,128)S(1)} %get-tuple-element.42), channel_id=1, source_target_pairs={{0,1},{1,2},{2,3},{3,4},{4,5},{5,6},{6,7},{7,8},{8,9},{9,10},{10,1... | collective-permute-start | bytes 1640 | tf_op jit(solution)/shard_map/ppermute | solution.py:18
  549.2 11.5 %collective-permute-start.79 = (f32[4,1,256]{2,1,0:T(1,128)S(1)}, f32[4,1,256]{2,1,0:T(1,128)S(1)}, u32[]{:S(2)}, u32[]{:S(2)}) collective-permute-start(f32[4,1,256]{2,1,0:T(1,128)S(1)} %get-tuple-element.72), channel_id=1, source_target_pairs={{16,0},{32,16},{48,32},{64,48},{80,64},{96,80},{112,96},{17,1},{33... | collective-permute-start | bytes 12296 | tf_op jit(solution)/shard_map/ppermute | solution.py:21
  579.3 19.0 %collective-permute-start.84 = (f32[4,1,256]{2,1,0:T(1,128)S(1)}, f32[4,1,256]{2,1,0:T(1,128)S(1)}, u32[]{:S(2)}, u32[]{:S(2)}) collective-permute-start(f32[4,1,256]{2,1,0:T(1,128)S(1)} %get-tuple-element.69), channel_id=1, source_target_pairs={{0,16},{16,32},{32,48},{48,64},{64,80},{80,96},{96,112},{1,17},{17... | collective-permute-start | bytes 12296 | tf_op jit(solution)/shard_map/ppermute | solution.py:18
  581.2 17.1 %collective-permute-start.85 = (f32[4,1,256]{2,1,0:T(1,128)S(1)}, f32[4,1,256]{2,1,0:T(1,128)S(1)}, u32[]{:S(2)}, u32[]{:S(2)}) collective-permute-start(f32[4,1,256]{2,1,0:T(1,128)S(1)} %get-tuple-element.70), channel_id=1, source_target_pairs={{16,0},{32,16},{48,32},{64,48},{80,64},{96,80},{112,96},{17,1},{33... | collective-permute-start | bytes 12296 | tf_op jit(solution)/shard_map/ppermute | solution.py:21
  598.5 14.2 %collective-permute-start.86 = (f32[4,34,1]{2,1,0:T(8,128)S(1)}, f32[4,34,1]{2,1,0:T(8,128)S(1)}, u32[]{:S(2)}, u32[]{:S(2)}) collective-permute-start(f32[4,34,1]{2,1,0:T(8,128)S(1)} %get-tuple-element.37), channel_id=1, source_target_pairs={{1,0},{2,1},{3,2},{4,3},{5,4},{6,5},{7,6},{8,7},{9,8},{10,9},{11,1... | collective-permute-start | bytes 1640 | tf_op jit(solution)/shard_map/ppermute | solution.py:21
  600.4 12.3 %collective-permute-start.87 = (f32[4,34,1]{2,1,0:T(8,128)S(1)}, f32[4,34,1]{2,1,0:T(8,128)S(1)}, u32[]{:S(2)}, u32[]{:S(2)}) collective-permute-start(f32[4,34,1]{2,1,0:T(8,128)S(1)} %get-tuple-element.38), channel_id=1, source_target_pairs={{0,1},{1,2},{2,3},{3,4},{4,5},{5,6},{6,7},{7,8},{8,9},{9,10},{10,1... | collective-permute-start | bytes 1640 | tf_op jit(solution)/shard_map/ppermute | solution.py:18
  602.8 12.6 %collective-permute-start.122 = (f32[1,256]{1,0:T(1,128)S(1)}, f32[1,256]{1,0:T(1,128)S(1)}, u32[]{:S(2)}, u32[]{:S(2)}) collective-permute-start(f32[1,256]{1,0:T(1,128)S(1)} %get-tuple-element.153), channel_id=1, source_target_pairs={{0,16},{16,32},{32,48},{48,64},{64,80},{80,96},{96,112},{1,17},{17... | collective-permute-start | bytes 3080 | tf_op jit(solution)/shard_map/ppermute | solution.py:18
  622.3 16.4 %collective-permute-start.90 = (f32[4,1,256]{2,1,0:T(1,128)S(1)}, f32[4,1,256]{2,1,0:T(1,128)S(1)}, u32[]{:S(2)}, u32[]{:S(2)}) collective-permute-start(f32[4,1,256]{2,1,0:T(1,128)S(1)} %get-tuple-element.67), channel_id=1, source_target_pairs={{0,16},{16,32},{32,48},{48,64},{64,80},{80,96},{96,112},{1,17},{17... | collective-permute-start | bytes 12296 | tf_op jit(solution)/shard_map/ppermute | solution.py:18
  629.9 11.5 %collective-permute-start.91 = (f32[4,1,256]{2,1,0:T(1,128)S(1)}, f32[4,1,256]{2,1,0:T(1,128)S(1)}, u32[]{:S(2)}, u32[]{:S(2)}) collective-permute-start(f32[4,1,256]{2,1,0:T(1,128)S(1)} %get-tuple-element.68), channel_id=1, source_target_pairs={{16,0},{32,16},{48,32},{64,48},{80,64},{96,80},{112,96},{17,1},{33... | collective-permute-start | bytes 12296 | tf_op jit(solution)/shard_map/ppermute | solution.py:21
  631.9 14.0 %collective-permute-start.124 = (f32[34,1]{1,0:T(8,128)S(1)}, f32[34,1]{1,0:T(8,128)S(1)}, u32[]{:S(2)}, u32[]{:S(2)}) collective-permute-start(f32[34,1]{1,0:T(8,128)S(1)} %get-tuple-element.144), channel_id=1, source_target_pairs={{0,1},{1,2},{2,3},{3,4},{4,5},{5,6},{6,7},{7,8},{8,9},{9,10},{10,1... | collective-permute-start | bytes 416 | tf_op jit(solution)/shard_map/ppermute | solution.py:18
  633.8 12.1 %collective-permute-start.125 = (f32[34,1]{1,0:T(8,128)S(1)}, f32[34,1]{1,0:T(8,128)S(1)}, u32[]{:S(2)}, u32[]{:S(2)}) collective-permute-start(f32[34,1]{1,0:T(8,128)S(1)} %get-tuple-element.143), channel_id=1, source_target_pairs={{1,0},{2,1},{3,2},{4,3},{5,4},{6,5},{7,6},{8,7},{9,8},{10,9},{11,1... | collective-permute-start | bytes 416 | tf_op jit(solution)/shard_map/ppermute | solution.py:21
  650.6 23.3 %collective-permute-start.98 = (f32[1,32,256]{2,1,0:T(8,128)S(1)}, f32[1,32,256]{2,1,0:T(8,128)S(1)}, u32[]{:S(2)}, u32[]{:S(2)}) collective-permute-start(f32[1,32,256]{2,1,0:T(8,128)S(1)} %get-tuple-element.110), channel_id=1, source_target_pairs={{0,128},{128,256},{256,384},{1,129},{129,257},{257,385},{2,130},{1... | collective-permute-start | bytes 98312 | tf_op jit(solution)/shard_map/ppermute | solution.py:18
  654.3 19.6 %collective-permute-start.99 = (f32[1,32,256]{2,1,0:T(8,128)S(1)}, f32[1,32,256]{2,1,0:T(8,128)S(1)}, u32[]{:S(2)}, u32[]{:S(2)}) collective-permute-start(f32[1,32,256]{2,1,0:T(8,128)S(1)} %get-tuple-element.111), channel_id=1, source_target_pairs={{128,0},{256,128},{384,256},{129,1},{257,129},{385,257},{130,2},{2... | collective-permute-start | bytes 98312 | tf_op jit(solution)/shard_map/ppermute | solution.py:21
  681.2 11.5 %collective-permute-start.101 = (f32[4,1,256]{2,1,0:T(1,128)S(1)}, f32[4,1,256]{2,1,0:T(1,128)S(1)}, u32[]{:S(2)}, u32[]{:S(2)}) collective-permute-start(f32[4,1,256]{2,1,0:T(1,128)S(1)} %get-tuple-element.66), channel_id=1, source_target_pairs={{16,0},{32,16},{48,32},{64,48},{80,64},{96,80},{112,96},{17,1},{33... | collective-permute-start | bytes 12296 | tf_op jit(solution)/shard_map/ppermute | solution.py:21
  692.8 17.5 %collective-permute-start.102 = (f32[4,34,1]{2,1,0:T(8,128)S(1)}, f32[4,34,1]{2,1,0:T(8,128)S(1)}, u32[]{:S(2)}, u32[]{:S(2)}) collective-permute-start(f32[4,34,1]{2,1,0:T(8,128)S(1)} %get-tuple-element.33), channel_id=1, source_target_pairs={{1,0},{2,1},{3,2},{4,3},{5,4},{6,5},{7,6},{8,7},{9,8},{10,9},{11,1... | collective-permute-start | bytes 1640 | tf_op jit(solution)/shard_map/ppermute | solution.py:21
  694.7 15.6 %collective-permute-start.103 = (f32[4,34,1]{2,1,0:T(8,128)S(1)}, f32[4,34,1]{2,1,0:T(8,128)S(1)}, u32[]{:S(2)}, u32[]{:S(2)}) collective-permute-start(f32[4,34,1]{2,1,0:T(8,128)S(1)} %get-tuple-element.34), channel_id=1, source_target_pairs={{0,1},{1,2},{2,3},{3,4},{4,5},{5,6},{6,7},{7,8},{8,9},{9,10},{10,1... | collective-permute-start | bytes 1640 | tf_op jit(solution)/shard_map/ppermute | solution.py:18
  751.6 11.5 %collective-permute-start.113 = (f32[4,1,256]{2,1,0:T(1,128)S(1)}, f32[4,1,256]{2,1,0:T(1,128)S(1)}, u32[]{:S(2)}, u32[]{:S(2)}) collective-permute-start(f32[4,1,256]{2,1,0:T(1,128)S(1)} %get-tuple-element.62), channel_id=1, source_target_pairs={{16,0},{32,16},{48,32},{64,48},{80,64},{96,80},{112,96},{17,1},{33... | collective-permute-start | bytes 12296 | tf_op jit(solution)/shard_map/ppermute | solution.py:21
  782.0 11.5 %collective-permute-start.119 = (f32[4,1,256]{2,1,0:T(1,128)S(1)}, f32[4,1,256]{2,1,0:T(1,128)S(1)}, u32[]{:S(2)}, u32[]{:S(2)}) collective-permute-start(f32[4,1,256]{2,1,0:T(1,128)S(1)} %get-tuple-element.60), channel_id=1, source_target_pairs={{16,0},{32,16},{48,32},{64,48},{80,64},{96,80},{112,96},{17,1},{33... | collective-permute-start | bytes 12296 | tf_op jit(solution)/shard_map/ppermute | solution.py:21
  793.6 17.5 %collective-permute-start.120 = (f32[4,34,1]{2,1,0:T(8,128)S(1)}, f32[4,34,1]{2,1,0:T(8,128)S(1)}, u32[]{:S(2)}, u32[]{:S(2)}) collective-permute-start(f32[4,34,1]{2,1,0:T(8,128)S(1)} %get-tuple-element.27), channel_id=1, source_target_pairs={{1,0},{2,1},{3,2},{4,3},{5,4},{6,5},{7,6},{8,7},{9,8},{10,9},{11,1... | collective-permute-start | bytes 1640 | tf_op jit(solution)/shard_map/ppermute | solution.py:21
  795.5 15.6 %collective-permute-start.121 = (f32[4,34,1]{2,1,0:T(8,128)S(1)}, f32[4,34,1]{2,1,0:T(8,128)S(1)}, u32[]{:S(2)}, u32[]{:S(2)}) collective-permute-start(f32[4,34,1]{2,1,0:T(8,128)S(1)} %get-tuple-element.28), channel_id=1, source_target_pairs={{0,1},{1,2},{2,3},{3,4},{4,5},{5,6},{6,7},{7,8},{8,9},{9,10},{10,1... | collective-permute-start | bytes 1640 | tf_op jit(solution)/shard_map/ppermute | solution.py:18
  (71 other events, 766.8 us)
Sparse Core Ops, SparseCore 0:
  115.2 56.7 all-reduce.2
where the time goes:
time: 824 us; the launch traced here: 819 us
  starting transfers between devices  379 us (46%)
  waiting for transfers between devices  229 us (28%)
  blocking collectives  161 us (20%)
  between operations  16.3 us (2%)
  local copies, waits for them, and re-layouts  13.5 us (2%)
  other arithmetic  11.3 us (1%)
  matrix products  9.98 us (1%)
    ppermute x63, starting transfers between devices, padded(): lax.ppermute(lax.slice_in_dim(block, block.shape[dim] - width, None, axis...  234 us
    ppermute x63, waiting for transfers between devices, padded(): lax.ppermute(lax.slice_in_dim(block, 0, width, axis=dim), axis, backward)  151 us
    ppermute x63, starting transfers between devices, padded(): lax.ppermute(lax.slice_in_dim(block, 0, width, axis=dim), axis, backward)  145 us
    psum x3, blocking collectives, spread(): return lax.psum(jnp.where(mine, value, jnp.zeros_like(value)), axis)  55.9 us
    all_gather x4, blocking collectives, shards(): lax.all_gather(source_strip, 'sec', axis=0, tiled=True)  52.7 us
    all_gather x4, blocking collectives, shards(): lax.all_gather(new_strip, 'sec', axis=0, tiled=True)  52.6 us
    psum x1, waiting for transfers between devices, spread(): return lax.psum(jnp.where(mine, value, jnp.zeros_like(value)), axis)  38.9 us
    ppermute x63, waiting for transfers between devices, padded(): lax.ppermute(lax.slice_in_dim(block, block.shape[dim] - width, None, axis...  38.6 us
  transfers between devices with their start and end apart: 127, of which 46 were waited for; matrix products, arithmetic and copies ran while one was open for 4% of the time, Pallas kernels for 0%

commit v1 on v0

--- a/solution.py
+++ b/solution.py
@@ -25,7 +25,8 @@
 
 def spread(value, axis, root):
     mine = lax.axis_index(axis) == root
-    return lax.psum(jnp.where(mine, value, jnp.zeros_like(value)), axis)
+    notes_spread = lambda mat, which_axis: jnp.sum(lax.all_gather(mat, which_axis), axis=0)
+    return notes_spread(jnp.where(mine, value, jnp.zeros_like(value)), which_axis=axis)
 
 
 def infiltration(land_frac, top_cond, surface, top_press):

time: 824 us -> 810 us (0.983)
  waiting for transfers between devices: 229 us -> 195 us
  blocking collectives: 161 us -> 178 us
  between operations: 16.3 us -> 3.1 us
  other arithmetic: 11.3 us -> 22.1 us
    all_gather x0 -> x5, blocking collectives: none -> 71.8 us  [spread(): lax.all_gather(mat, which_axis)]
    psum x3 -> x0, blocking collectives: 55.9 us -> none  [spread(): return lax.psum(jnp.where(mine, value, jnp.zeros_like(value)), axis)]
    psum x1 -> x0, waiting for transfers between devices: 38.9 us -> none  [spread(): return lax.psum(jnp.where(mine, value, jnp.zeros_like(value)), axis)]
    div x16, other arithmetic: 2.83 us -> 11.3 us  [jacobi_sweep(): return total / diagonal]
  transfers between devices with their start and end apart: 127 -> 126, of which waited for: 46 -> 45; matrix products, arithmetic and copies ran while one was open for 4% -> 4% of each run, Pallas kernels for 0% -> 0%
where the time goes in v1:
time: 810 us; the launch traced here: 806 us
  starting transfers between devices  380 us (47%)
  waiting for transfers between devices  195 us (24%)
  blocking collectives  178 us (22%)
  other arithmetic  22.1 us (3%)
  local copies, waits for them, and re-layouts  18.1 us (2%)
  matrix products  9.32 us (1%)
    ppermute x63, starting transfers between devices, padded(): lax.ppermute(lax.slice_in_dim(block, block.shape[dim] - width, None, axis...  234 us
    ppermute x63, waiting for transfers between devices, padded(): lax.ppermute(lax.slice_in_dim(block, 0, width, axis=dim), axis, backward)  154 us
    ppermute x63, starting transfers between devices, padded(): lax.ppermute(lax.slice_in_dim(block, 0, width, axis=dim), axis, backward)  146 us
    all_gather x5, blocking collectives, spread(): lax.all_gather(mat, which_axis)  71.8 us
    all_gather x4, blocking collectives, shards(): lax.all_gather(source_strip, 'sec', axis=0, tiled=True)  53.8 us
    all_gather x4, blocking collectives, shards(): lax.all_gather(new_strip, 'sec', axis=0, tiled=True)  52.6 us
    ppermute x63, waiting for transfers between devices, padded(): lax.ppermute(lax.slice_in_dim(block, block.shape[dim] - width, None, axis...  41.3 us
  transfers between devices with their start and end apart: 126, of which 45 were waited for; matrix products, arithmetic and copies ran while one was open for 4% of the time, Pallas kernels for 0%

profile of v1, /device:TPU:38, one launch (start us, length us, event | category | flops | bytes accessed | tf_op | source)
XLA Modules:
  0.0 806.0 jit_solution(17257284937519495224)
XLA Ops:
  1.5 10.8 %collective-permute-start = (s32[2,1,256]{2,1,0:T(1,128)S(1)}, s32[2,1,256]{2,1,0:T(1,128)S(1)}, u32[]{:S(2)}, u32[]{:S(2)}) collective-permute-start(s32[2,1,256]{2,1,0:T(1,128)S(1)} %get-tuple-element.145), channel_id=1, source_target_pairs={{0,16},{16,32},{32,48},{48,64},{64,80},{80,96},{96,112},{1,17},{17... | collective-permute-start | bytes 6152 | tf_op jit(solution)/shard_map/ppermute | solution.py:18
  15.1 9.9 %collective-permute-start.38 = (f32[1,256]{1,0:T(1,128)S(1)}, f32[1,256]{1,0:T(1,128)S(1)}, u32[]{:S(2)}, u32[]{:S(2)}) collective-permute-start(f32[1,256]{1,0:T(1,128)S(1)} %get-tuple-element.165), channel_id=1, source_target_pairs={{0,16},{16,32},{32,48},{48,64},{64,80},{80,96},{96,112},{1,17},{17... | collective-permute-start | bytes 3080 | tf_op jit(solution)/shard_map/ppermute | solution.py:18
  27.7 9.9 %collective-permute-start.34 = (f32[1,256]{1,0:T(1,128)S(1)}, f32[1,256]{1,0:T(1,128)S(1)}, u32[]{:S(2)}, u32[]{:S(2)}) collective-permute-start(f32[1,256]{1,0:T(1,128)S(1)} %get-tuple-element.163), channel_id=1, source_target_pairs={{0,16},{16,32},{32,48},{48,64},{64,80},{80,96},{96,112},{1,17},{17... | collective-permute-start | bytes 3080 | tf_op jit(solution)/shard_map/ppermute | solution.py:18
  39.3 13.4 %all_gather.45 = f32[4,32,256]{2,1,0:T(8,128)S(1)} all-gather(f32[1,32,256]{2,1,0:T(8,128)S(1)} %copy.57), channel_id=1, replica_groups=mesh['sec'=4,'gx'=8,'gy'=16] {'sec'}, dimensions={0}, use_global_device_ids=true | all-gather | bytes 163840 | tf_op jit(solution)/shard_map/all_gather | solution.py:28
  62.2 6.2 collective-permute-done.35
  76.6 4.6 collective-permute-start.37
  83.3 4.9 collective-permute-start.3
  98.6 5.4 maximum_convert_fusion
  110.4 13.4 %all_gather.44 = f32[4,32,256]{2,1,0:T(8,128)S(1)} all-gather(f32[1,32,256]{2,1,0:T(8,128)S(1)} %copy.55), channel_id=1, replica_groups=mesh['sec'=4,'gx'=8,'gy'=16] {'sec'}, dimensions={0}, use_global_device_ids=true | all-gather | bytes 163840 | tf_op jit(solution)/shard_map/all_gather | solution.py:28
  127.6 14.4 %all_gather.46 = f32[32,256]{1,0:T(8,128)S(1)} all-gather(f32[8,256]{1,0:T(8,128)S(1)} %get-tuple-element.28), channel_id=1, replica_groups=mesh['sec'=4,'gx'=8,'gy'=16] {'sec'}, dimensions={0}, use_global_device_ids=true | all-gather | bytes 40960 | tf_op jit(solution)/shard_map/all_gather | solution.py:167
  142.1 7.8 collective-permute-start.12
  151.8 9.9 %collective-permute-start.6 = (f32[2,4,1,256]{3,1,2,0:T(4,128)S(1)}, f32[2,4,1,256]{3,1,2,0:T(4,128)S(1)}, u32[]{:S(2)}, u32[]{:S(2)}) collective-permute-start(f32[2,4,1,256]{3,1,2,0:T(4,128)S(1)} %get-tuple-element.32), channel_id=1, source_target_pairs={{0,16},{16,32},{32,48},{48,64},{64,80},{80,96},{96,112},{1,17},{17... | collective-permute-start | bytes 24584 | tf_op jit(solution)/shard_map/ppermute | solution.py:18
  163.8 9.5 %collective-permute-done.7 = f32[2,4,1,256]{3,1,2,0:T(4,128)S(1)} collective-permute-done((f32[2,4,1,256]{3,1,2,0:T(4,128)S(1)}, f32[2,4,1,256]{3,1,2,0:T(4,128)S(1)}, u32[]{:S(2)}, u32[]{:S(2)}) %collective-permute-start.7) | collective-permute-done | bytes 8224 | tf_op jit(solution)/shard_map/ppermute | solution.py:21
  175.6 4.9 collective-permute-start.9
  196.7 4.2 collective-permute-done.17
  206.8 7.6 collective-permute-done.19
  218.9 4.4 collective-permute-done.21
  228.5 4.2 collective-permute-done.23
  238.6 13.1 %all_gather.47 = f32[32,256]{1,0:T(8,128)S(1)} all-gather(f32[8,256]{1,0:T(8,128)S(1)} %get-tuple-element.14), channel_id=1, replica_groups=mesh['sec'=4,'gx'=8,'gy'=16] {'sec'}, dimensions={0}, use_global_device_ids=true | all-gather | bytes 40960 | tf_op jit(solution)/shard_map/all_gather | solution.py:166
  256.3 7.9 collective-permute-start.66
  270.3 5.4 collective-permute-done.67
  275.8 9.0 %collective-permute-start.30 = (f32[4,1,256]{2,0,1:T(4,128)S(1)}, f32[4,1,256]{2,0,1:T(4,128)S(1)}, u32[]{:S(2)}, u32[]{:S(2)}) collective-permute-start(f32[4,1,256]{2,0,1:T(4,128)S(1)} %get-tuple-element.90), channel_id=1, source_target_pairs={{0,16},{16,32},{32,48},{48,64},{64,80},{80,96},{96,112},{1,17},{17... | collective-permute-start | bytes 12296 | tf_op jit(solution)/shard_map/ppermute | solution.py:18
  288.7 4.9 collective-permute-start.69
  300.9 4.3 collective-permute-done.33
  310.1 15.2 %all_gather.48 = f32[4,32,256]{2,1,0:T(8,128)S(1)} all-gather(f32[1,32,256]{2,1,0:T(8,128)S(1)} %copy.65), channel_id=1, replica_groups=mesh['sec'=4,'gx'=8,'gy'=16] {'sec'}, dimensions={0}, use_global_device_ids=true | all-gather | bytes 163840 | tf_op jit(solution)/shard_map/all_gather | solution.py:28
  325.3 7.1 collective-permute-start.44
  334.5 9.5 %collective-permute-done.45 = f32[4,1,256]{2,0,1:T(4,128)S(1)} collective-permute-done((f32[4,1,256]{2,0,1:T(4,128)S(1)}, f32[4,1,256]{2,0,1:T(4,128)S(1)}, u32[]{:S(2)}, u32[]{:S(2)}) %collective-permute-start.45) | collective-permute-done | bytes 4128 | tf_op jit(solution)/shard_map/ppermute | solution.py:21
  348.5 13.1 %all_gather.49 = f32[32,256]{1,0:T(8,128)S(1)} all-gather(f32[8,256]{1,0:T(8,128)S(1)} %get-tuple-element.109), channel_id=1, replica_groups=mesh['sec'=4,'gx'=8,'gy'=16] {'sec'}, dimensions={0}, use_global_device_ids=true | all-gather | bytes 40960 | tf_op jit(solution)/shard_map/all_gather | solution.py:167
  365.9 4.3 collective-permute-done.49
  376.0 7.6 collective-permute-done.51
  388.2 4.4 collective-permute-done.53
  397.8 4.2 collective-permute-done.55
  407.9 13.1 %all_gather.50 = f32[32,256]{1,0:T(8,128)S(1)} all-gather(f32[8,256]{1,0:T(8,128)S(1)} %get-tuple-element.108), channel_id=1, replica_groups=mesh['sec'=4,'gx'=8,'gy'=16] {'sec'}, dimensions={0}, use_global_device_ids=true | all-gather | bytes 40960 | tf_op jit(solution)/shard_map/all_gather | solution.py:166
  425.6 7.9 collective-permute-start.94
  439.4 5.6 collective-permute-done.95
  445.1 8.8 %collective-permute-start.62 = (f32[4,1,256]{2,0,1:T(4,128)S(1)}, f32[4,1,256]{2,0,1:T(4,128)S(1)}, u32[]{:S(2)}, u32[]{:S(2)}) collective-permute-start(f32[4,1,256]{2,0,1:T(4,128)S(1)} %get-tuple-element.82), channel_id=1, source_target_pairs={{0,16},{16,32},{32,48},{48,64},{64,80},{80,96},{96,112},{1,17},{17... | collective-permute-start | bytes 12296 | tf_op jit(solution)/shard_map/ppermute | solution.py:18
  457.8 4.9 collective-permute-start.97
  470.1 4.3 collective-permute-done.65
  479.5 14.9 %all_gather.51 = f32[4,32,256]{2,1,0:T(8,128)S(1)} all-gather(f32[1,32,256]{2,1,0:T(8,128)S(1)} %copy.67), channel_id=1, replica_groups=mesh['sec'=4,'gx'=8,'gy'=16] {'sec'}, dimensions={0}, use_global_device_ids=true | all-gather | bytes 163840 | tf_op jit(solution)/shard_map/all_gather | solution.py:28
  494.5 7.1 collective-permute-start.72
  503.8 9.3 %collective-permute-done.73 = f32[4,1,256]{2,0,1:T(4,128)S(1)} collective-permute-done((f32[4,1,256]{2,0,1:T(4,128)S(1)}, f32[4,1,256]{2,0,1:T(4,128)S(1)}, u32[]{:S(2)}, u32[]{:S(2)}) %collective-permute-start.73) | collective-permute-done | bytes 4128 | tf_op jit(solution)/shard_map/ppermute | solution.py:21
  517.6 13.1 %all_gather.52 = f32[32,256]{1,0:T(8,128)S(1)} all-gather(f32[8,256]{1,0:T(8,128)S(1)} %get-tuple-element.107), channel_id=1, replica_groups=mesh['sec'=4,'gx'=8,'gy'=16] {'sec'}, dimensions={0}, use_global_device_ids=true | all-gather | bytes 40960 | tf_op jit(solution)/shard_map/all_gather | solution.py:167
  535.0 4.3 collective-permute-done.77
  545.2 7.6 collective-permute-done.79
  557.3 4.4 collective-permute-done.81
  566.9 4.2 collective-permute-done.83
  577.0 13.1 %all_gather.53 = f32[32,256]{1,0:T(8,128)S(1)} all-gather(f32[8,256]{1,0:T(8,128)S(1)} %get-tuple-element.106), channel_id=1, replica_groups=mesh['sec'=4,'gx'=8,'gy'=16] {'sec'}, dimensions={0}, use_global_device_ids=true | all-gather | bytes 40960 | tf_op jit(solution)/shard_map/all_gather | solution.py:166
  594.8 7.9 collective-permute-start.122
  608.6 5.6 collective-permute-done.123
  614.3 8.8 %collective-permute-start.90 = (f32[4,1,256]{2,0,1:T(4,128)S(1)}, f32[4,1,256]{2,0,1:T(4,128)S(1)}, u32[]{:S(2)}, u32[]{:S(2)}) collective-permute-start(f32[4,1,256]{2,0,1:T(4,128)S(1)} %get-tuple-element.74), channel_id=1, source_target_pairs={{0,16},{16,32},{32,48},{48,64},{64,80},{80,96},{96,112},{1,17},{17... | collective-permute-start | bytes 12296 | tf_op jit(solution)/shard_map/ppermute | solution.py:18
  627.0 4.9 collective-permute-start.125
  639.2 4.3 collective-permute-done.93
  648.6 14.9 %all_gather.54 = f32[4,32,256]{2,1,0:T(8,128)S(1)} all-gather(f32[1,32,256]{2,1,0:T(8,128)S(1)} %copy.69), channel_id=1, replica_groups=mesh['sec'=4,'gx'=8,'gy'=16] {'sec'}, dimensions={0}, use_global_device_ids=true | all-gather | bytes 163840 | tf_op jit(solution)/shard_map/all_gather | solution.py:28
  663.6 7.1 collective-permute-start.100
  672.7 9.5 %collective-permute-done.101 = f32[4,1,256]{2,0,1:T(4,128)S(1)} collective-permute-done((f32[4,1,256]{2,0,1:T(4,128)S(1)}, f32[4,1,256]{2,0,1:T(4,128)S(1)}, u32[]{:S(2)}, u32[]{:S(2)}) %collective-permute-start.101) | collective-permute-done | bytes 4128 | tf_op jit(solution)/shard_map/ppermute | solution.py:21
  686.8 13.1 %all_gather.55 = f32[32,256]{1,0:T(8,128)S(1)} all-gather(f32[8,256]{1,0:T(8,128)S(1)} %get-tuple-element.105), channel_id=1, replica_groups=mesh['sec'=4,'gx'=8,'gy'=16] {'sec'}, dimensions={0}, use_global_device_ids=true | all-gather | bytes 40960 | tf_op jit(solution)/shard_map/all_gather | solution.py:167
  704.1 4.3 collective-permute-done.105
  714.3 7.6 collective-permute-done.107
  726.4 4.4 collective-permute-done.109
  746.2 7.6 collective-permute-done.113
  758.3 4.4 collective-permute-done.115
  768.7 4.2 collective-permute-done.117
  778.8 7.6 collective-permute-done.119
  790.9 13.2 %all_gather.56 = f32[32,256]{1,0:T(8,128)S(1)} all-gather(f32[8,256]{1,0:T(8,128)S(1)} %get-tuple-element.104), channel_id=1, replica_groups=mesh['sec'=4,'gx'=8,'gy'=16] {'sec'}, dimensions={0}, use_global_device_ids=true | all-gather | bytes 40960 | tf_op jit(solution)/shard_map/all_gather | solution.py:166
  (384 shorter events, 295.3 us)
Async XLA Ops:
  1.5 75.1 %collective-permute-start = (s32[2,1,256]{2,1,0:T(1,128)S(1)}, s32[2,1,256]{2,1,0:T(1,128)S(1)}, u32[]{:S(2)}, u32[]{:S(2)}) collective-permute-start(s32[2,1,256]{2,1,0:T(1,128)S(1)} %get-tuple-element.145), channel_id=1, source_target_pairs={{0,16},{16,32},{32,48},{48,64},{64,80},{80,96},{96,112},{1,17},{17... | collective-permute-start | bytes 6152 | tf_op jit(solution)/shard_map/ppermute | solution.py:18
  12.3 68.9 %collective-permute-start.1 = (s32[2,1,256]{2,1,0:T(1,128)S(1)}, s32[2,1,256]{2,1,0:T(1,128)S(1)}, u32[]{:S(2)}, u32[]{:S(2)}) collective-permute-start(s32[2,1,256]{2,1,0:T(1,128)S(1)} %get-tuple-element.146), channel_id=1, source_target_pairs={{16,0},{32,16},{48,32},{64,48},{80,64},{96,80},{112,96},{17,1},{33... | collective-permute-start | bytes 6152 | tf_op jit(solution)/shard_map/ppermute | solution.py:21
  15.1 41.9 %collective-permute-start.38 = (f32[1,256]{1,0:T(1,128)S(1)}, f32[1,256]{1,0:T(1,128)S(1)}, u32[]{:S(2)}, u32[]{:S(2)}) collective-permute-start(f32[1,256]{1,0:T(1,128)S(1)} %get-tuple-element.165), channel_id=1, source_target_pairs={{0,16},{16,32},{32,48},{48,64},{64,80},{80,96},{96,112},{1,17},{17... | collective-permute-start | bytes 3080 | tf_op jit(solution)/shard_map/ppermute | solution.py:18
  25.0 33.8 %collective-permute-start.39 = (f32[1,256]{1,0:T(1,128)S(1)}, f32[1,256]{1,0:T(1,128)S(1)}, u32[]{:S(2)}, u32[]{:S(2)}) collective-permute-start(f32[1,256]{1,0:T(1,128)S(1)} %get-tuple-element.166), channel_id=1, source_target_pairs={{16,0},{32,16},{48,32},{64,48},{80,64},{96,80},{112,96},{17,1},{33... | collective-permute-start | bytes 3080 | tf_op jit(solution)/shard_map/ppermute | solution.py:21
  27.7 32.5 %collective-permute-start.34 = (f32[1,256]{1,0:T(1,128)S(1)}, f32[1,256]{1,0:T(1,128)S(1)}, u32[]{:S(2)}, u32[]{:S(2)}) collective-permute-start(f32[1,256]{1,0:T(1,128)S(1)} %get-tuple-element.163), channel_id=1, source_target_pairs={{0,16},{16,32},{32,48},{48,64},{64,80},{80,96},{96,112},{1,17},{17... | collective-permute-start | bytes 3080 | tf_op jit(solution)/shard_map/ppermute | solution.py:18
  58.8 83.2 %collective-permute-start.11 = (f32[1,32,256]{2,0,1:T(1,128)}, f32[1,32,256]{2,0,1:T(1,128)S(1)}, u32[]{:S(2)}, u32[]{:S(2)}) collective-permute-start(f32[1,32,256]{2,0,1:T(1,128)} %get-tuple-element.144), channel_id=1, source_target_pairs={{128,0},{256,128},{384,256},{129,1},{257,129},{385,257},{130,2},{2... | collective-permute-start | bytes 98312 | tf_op jit(solution)/shard_map/ppermute | solution.py:21
  70.4 71.6 %collective-permute-start.10 = (f32[1,32,256]{2,0,1:T(1,128)}, f32[1,32,256]{2,0,1:T(1,128)S(1)}, u32[]{:S(2)}, u32[]{:S(2)}) collective-permute-start(f32[1,32,256]{2,0,1:T(1,128)} %copy.59), channel_id=1, source_target_pairs={{0,128},{128,256},{256,384},{1,129},{129,257},{257,385},{2,130},{1... | collective-permute-start | bytes 98312 | tf_op jit(solution)/shard_map/ppermute | solution.py:18
  76.6 11.5 %collective-permute-start.37 = (f32[34,1]{1,0:T(8,128)S(1)}, f32[34,1]{1,0:T(8,128)S(1)}, u32[]{:S(2)}, u32[]{:S(2)}) collective-permute-start(f32[34,1]{1,0:T(8,128)S(1)} %get-tuple-element.153), channel_id=1, source_target_pairs={{1,0},{2,1},{3,2},{4,3},{5,4},{6,5},{7,6},{8,7},{9,8},{10,9},{11,1... | collective-permute-start | bytes 416 | tf_op jit(solution)/shard_map/ppermute | solution.py:21
  123.9 27.9 %collective-permute-start.4 = (f32[2,1,32,256]{3,1,2,0:T(1,128)S(1)}, f32[2,1,32,256]{3,1,2,0:T(1,128)S(1)}, u32[]{:S(2)}, u32[]{:S(2)}) collective-permute-start(f32[2,1,32,256]{3,1,2,0:T(1,128)S(1)} %get-tuple-element.96), channel_id=1, source_target_pairs={{0,128},{128,256},{256,384},{1,129},{129,257},{257,385},{2,130},{1... | collective-permute-start | bytes 196616 | tf_op jit(solution)/shard_map/ppermute | solution.py:18
  125.4 26.4 %collective-permute-start.5 = (f32[2,1,32,256]{3,1,2,0:T(1,128)S(1)}, f32[2,1,32,256]{3,1,2,0:T(1,128)S(1)}, u32[]{:S(2)}, u32[]{:S(2)}) collective-permute-start(f32[2,1,32,256]{3,1,2,0:T(1,128)S(1)} %get-tuple-element.97), channel_id=1, source_target_pairs={{128,0},{256,128},{384,256},{129,1},{257,129},{385,257},{130,2},{2... | collective-permute-start | bytes 196616 | tf_op jit(solution)/shard_map/ppermute | solution.py:21
  142.1 21.6 %collective-permute-start.12 = (f32[4,1,256]{2,0,1:T(4,128)S(1)}, f32[4,1,256]{2,0,1:T(4,128)S(1)}, u32[]{:S(2)}, u32[]{:S(2)}) collective-permute-start(f32[4,1,256]{2,0,1:T(4,128)S(1)} %get-tuple-element.98), channel_id=1, source_target_pairs={{0,16},{16,32},{32,48},{48,64},{64,80},{80,96},{96,112},{1,17},{17... | collective-permute-start | bytes 12296 | tf_op jit(solution)/shard_map/ppermute | solution.py:18
  149.8 13.9 %collective-permute-start.13 = (f32[4,1,256]{2,0,1:T(4,128)S(1)}, f32[4,1,256]{2,0,1:T(4,128)S(1)}, u32[]{:S(2)}, u32[]{:S(2)}) collective-permute-start(f32[4,1,256]{2,0,1:T(4,128)S(1)} %get-tuple-element.99), channel_id=1, source_target_pairs={{16,0},{32,16},{48,32},{64,48},{80,64},{96,80},{112,96},{17,1},{33... | collective-permute-start | bytes 12296 | tf_op jit(solution)/shard_map/ppermute | solution.py:21
  151.8 12.0 %collective-permute-start.6 = (f32[2,4,1,256]{3,1,2,0:T(4,128)S(1)}, f32[2,4,1,256]{3,1,2,0:T(4,128)S(1)}, u32[]{:S(2)}, u32[]{:S(2)}) collective-permute-start(f32[2,4,1,256]{3,1,2,0:T(4,128)S(1)} %get-tuple-element.32), channel_id=1, source_target_pairs={{0,16},{16,32},{32,48},{48,64},{64,80},{80,96},{96,112},{1,17},{17... | collective-permute-start | bytes 24584 | tf_op jit(solution)/shard_map/ppermute | solution.py:18
  161.8 11.6 %collective-permute-start.7 = (f32[2,4,1,256]{3,1,2,0:T(4,128)S(1)}, f32[2,4,1,256]{3,1,2,0:T(4,128)S(1)}, u32[]{:S(2)}, u32[]{:S(2)}) collective-permute-start(f32[2,4,1,256]{3,1,2,0:T(4,128)S(1)} %get-tuple-element.33), channel_id=1, source_target_pairs={{16,0},{32,16},{48,32},{64,48},{80,64},{96,80},{112,96},{17,1},{33... | collective-permute-start | bytes 24584 | tf_op jit(solution)/shard_map/ppermute | solution.py:21
  202.9 11.5 %collective-permute-start.19 = (f32[4,1,256]{2,0,1:T(4,128)S(1)}, f32[4,1,256]{2,0,1:T(4,128)S(1)}, u32[]{:S(2)}, u32[]{:S(2)}) collective-permute-start(f32[4,1,256]{2,0,1:T(4,128)S(1)} %get-tuple-element.95), channel_id=1, source_target_pairs={{16,0},{32,16},{48,32},{64,48},{80,64},{96,80},{112,96},{17,1},{33... | collective-permute-start | bytes 12296 | tf_op jit(solution)/shard_map/ppermute | solution.py:21
  232.7 19.0 %collective-permute-start.24 = (f32[4,1,256]{2,0,1:T(4,128)S(1)}, f32[4,1,256]{2,0,1:T(4,128)S(1)}, u32[]{:S(2)}, u32[]{:S(2)}) collective-permute-start(f32[4,1,256]{2,0,1:T(4,128)S(1)} %get-tuple-element.92), channel_id=1, source_target_pairs={{0,16},{16,32},{32,48},{48,64},{64,80},{80,96},{96,112},{1,17},{17... | collective-permute-start | bytes 12296 | tf_op jit(solution)/shard_map/ppermute | solution.py:18
  234.6 17.1 %collective-permute-start.25 = (f32[4,1,256]{2,0,1:T(4,128)S(1)}, f32[4,1,256]{2,0,1:T(4,128)S(1)}, u32[]{:S(2)}, u32[]{:S(2)}) collective-permute-start(f32[4,1,256]{2,0,1:T(4,128)S(1)} %get-tuple-element.93), channel_id=1, source_target_pairs={{16,0},{32,16},{48,32},{64,48},{80,64},{96,80},{112,96},{17,1},{33... | collective-permute-start | bytes 12296 | tf_op jit(solution)/shard_map/ppermute | solution.py:21
  251.9 14.2 %collective-permute-start.26 = (f32[4,34,1]{2,0,1:T(4,128)S(1)}, f32[4,34,1]{2,0,1:T(4,128)S(1)}, u32[]{:S(2)}, u32[]{:S(2)}) collective-permute-start(f32[4,34,1]{2,0,1:T(4,128)S(1)} %get-tuple-element.60), channel_id=1, source_target_pairs={{1,0},{2,1},{3,2},{4,3},{5,4},{6,5},{7,6},{8,7},{9,8},{10,9},{11,1... | collective-permute-start | bytes 1640 | tf_op jit(solution)/shard_map/ppermute | solution.py:21
  253.9 12.3 %collective-permute-start.27 = (f32[4,34,1]{2,0,1:T(4,128)S(1)}, f32[4,34,1]{2,0,1:T(4,128)S(1)}, u32[]{:S(2)}, u32[]{:S(2)}) collective-permute-start(f32[4,34,1]{2,0,1:T(4,128)S(1)} %get-tuple-element.61), channel_id=1, source_target_pairs={{0,1},{1,2},{2,3},{3,4},{4,5},{5,6},{6,7},{7,8},{8,9},{9,10},{10,1... | collective-permute-start | bytes 1640 | tf_op jit(solution)/shard_map/ppermute | solution.py:18
  256.3 14.0 %collective-permute-start.66 = (f32[1,256]{1,0:T(1,128)S(1)}, f32[1,256]{1,0:T(1,128)S(1)}, u32[]{:S(2)}, u32[]{:S(2)}) collective-permute-start(f32[1,256]{1,0:T(1,128)S(1)} %get-tuple-element.161), channel_id=1, source_target_pairs={{0,16},{16,32},{32,48},{48,64},{64,80},{80,96},{96,112},{1,17},{17... | collective-permute-start | bytes 3080 | tf_op jit(solution)/shard_map/ppermute | solution.py:18
  275.8 17.7 %collective-permute-start.30 = (f32[4,1,256]{2,0,1:T(4,128)S(1)}, f32[4,1,256]{2,0,1:T(4,128)S(1)}, u32[]{:S(2)}, u32[]{:S(2)}) collective-permute-start(f32[4,1,256]{2,0,1:T(4,128)S(1)} %get-tuple-element.90), channel_id=1, source_target_pairs={{0,16},{16,32},{32,48},{48,64},{64,80},{80,96},{96,112},{1,17},{17... | collective-permute-start | bytes 12296 | tf_op jit(solution)/shard_map/ppermute | solution.py:18
  284.7 11.5 %collective-permute-start.31 = (f32[4,1,256]{2,0,1:T(4,128)S(1)}, f32[4,1,256]{2,0,1:T(4,128)S(1)}, u32[]{:S(2)}, u32[]{:S(2)}) collective-permute-start(f32[4,1,256]{2,0,1:T(4,128)S(1)} %get-tuple-element.91), channel_id=1, source_target_pairs={{16,0},{32,16},{48,32},{64,48},{80,64},{96,80},{112,96},{17,1},{33... | collective-permute-start | bytes 12296 | tf_op jit(solution)/shard_map/ppermute | solution.py:21
  286.8 14.1 %collective-permute-start.68 = (f32[34,1]{1,0:T(8,128)S(1)}, f32[34,1]{1,0:T(8,128)S(1)}, u32[]{:S(2)}, u32[]{:S(2)}) collective-permute-start(f32[34,1]{1,0:T(8,128)S(1)} %get-tuple-element.152), channel_id=1, source_target_pairs={{0,1},{1,2},{2,3},{3,4},{4,5},{5,6},{6,7},{7,8},{8,9},{9,10},{10,1... | collective-permute-start | bytes 416 | tf_op jit(solution)/shard_map/ppermute | solution.py:18
  288.7 12.1 %collective-permute-start.69 = (f32[34,1]{1,0:T(8,128)S(1)}, f32[34,1]{1,0:T(8,128)S(1)}, u32[]{:S(2)}, u32[]{:S(2)}) collective-permute-start(f32[34,1]{1,0:T(8,128)S(1)} %get-tuple-element.151), channel_id=1, source_target_pairs={{1,0},{2,1},{3,2},{4,3},{5,4},{6,5},{7,6},{8,7},{9,8},{10,9},{11,1... | collective-permute-start | bytes 416 | tf_op jit(solution)/shard_map/ppermute | solution.py:21
  305.9 19.4 %collective-permute-start.42 = (f32[1,32,256]{2,0,1:T(1,128)S(1)}, f32[1,32,256]{2,0,1:T(1,128)S(1)}, u32[]{:S(2)}, u32[]{:S(2)}) collective-permute-start(f32[1,32,256]{2,0,1:T(1,128)S(1)} %get-tuple-element.135), channel_id=1, source_target_pairs={{0,128},{128,256},{256,384},{1,129},{129,257},{257,385},{2,130},{1... | collective-permute-start | bytes 98312 | tf_op jit(solution)/shard_map/ppermute | solution.py:18
  308.8 16.5 %collective-permute-start.43 = (f32[1,32,256]{2,0,1:T(1,128)S(1)}, f32[1,32,256]{2,0,1:T(1,128)S(1)}, u32[]{:S(2)}, u32[]{:S(2)}) collective-permute-start(f32[1,32,256]{2,0,1:T(1,128)S(1)} %get-tuple-element.136), channel_id=1, source_target_pairs={{128,0},{256,128},{384,256},{129,1},{257,129},{385,257},{130,2},{2... | collective-permute-start | bytes 98312 | tf_op jit(solution)/shard_map/ppermute | solution.py:21
  332.4 11.5 %collective-permute-start.45 = (f32[4,1,256]{2,0,1:T(4,128)S(1)}, f32[4,1,256]{2,0,1:T(4,128)S(1)}, u32[]{:S(2)}, u32[]{:S(2)}) collective-permute-start(f32[4,1,256]{2,0,1:T(4,128)S(1)} %get-tuple-element.89), channel_id=1, source_target_pairs={{16,0},{32,16},{48,32},{64,48},{80,64},{96,80},{112,96},{17,1},{33... | collective-permute-start | bytes 12296 | tf_op jit(solution)/shard_map/ppermute | solution.py:21
  344.1 17.5 %collective-permute-start.46 = (f32[4,34,1]{2,0,1:T(4,128)S(1)}, f32[4,34,1]{2,0,1:T(4,128)S(1)}, u32[]{:S(2)}, u32[]{:S(2)}) collective-permute-start(f32[4,34,1]{2,0,1:T(4,128)S(1)} %get-tuple-element.56), channel_id=1, source_target_pairs={{1,0},{2,1},{3,2},{4,3},{5,4},{6,5},{7,6},{8,7},{9,8},{10,9},{11,1... | collective-permute-start | bytes 1640 | tf_op jit(solution)/shard_map/ppermute | solution.py:21
  346.1 15.6 %collective-permute-start.47 = (f32[4,34,1]{2,0,1:T(4,128)S(1)}, f32[4,34,1]{2,0,1:T(4,128)S(1)}, u32[]{:S(2)}, u32[]{:S(2)}) collective-permute-start(f32[4,34,1]{2,0,1:T(4,128)S(1)} %get-tuple-element.57), channel_id=1, source_target_pairs={{0,1},{1,2},{2,3},{3,4},{4,5},{5,6},{6,7},{7,8},{8,9},{9,10},{10,1... | collective-permute-start | bytes 1640 | tf_op jit(solution)/shard_map/ppermute | solution.py:18
  372.1 11.5 %collective-permute-start.51 = (f32[4,1,256]{2,0,1:T(4,128)S(1)}, f32[4,1,256]{2,0,1:T(4,128)S(1)}, u32[]{:S(2)}, u32[]{:S(2)}) collective-permute-start(f32[4,1,256]{2,0,1:T(4,128)S(1)} %get-tuple-element.87), channel_id=1, source_target_pairs={{16,0},{32,16},{48,32},{64,48},{80,64},{96,80},{112,96},{17,1},{33... | collective-permute-start | bytes 12296 | tf_op jit(solution)/shard_map/ppermute | solution.py:21
  402.0 19.0 %collective-permute-start.56 = (f32[4,1,256]{2,0,1:T(4,128)S(1)}, f32[4,1,256]{2,0,1:T(4,128)S(1)}, u32[]{:S(2)}, u32[]{:S(2)}) collective-permute-start(f32[4,1,256]{2,0,1:T(4,128)S(1)} %get-tuple-element.84), channel_id=1, source_target_pairs={{0,16},{16,32},{32,48},{48,64},{64,80},{80,96},{96,112},{1,17},{17... | collective-permute-start | bytes 12296 | tf_op jit(solution)/shard_map/ppermute | solution.py:18
  404.0 17.1 %collective-permute-start.57 = (f32[4,1,256]{2,0,1:T(4,128)S(1)}, f32[4,1,256]{2,0,1:T(4,128)S(1)}, u32[]{:S(2)}, u32[]{:S(2)}) collective-permute-start(f32[4,1,256]{2,0,1:T(4,128)S(1)} %get-tuple-element.85), channel_id=1, source_target_pairs={{16,0},{32,16},{48,32},{64,48},{80,64},{96,80},{112,96},{17,1},{33... | collective-permute-start | bytes 12296 | tf_op jit(solution)/shard_map/ppermute | solution.py:21
  421.3 14.2 %collective-permute-start.58 = (f32[4,34,1]{2,0,1:T(4,128)S(1)}, f32[4,34,1]{2,0,1:T(4,128)S(1)}, u32[]{:S(2)}, u32[]{:S(2)}) collective-permute-start(f32[4,34,1]{2,0,1:T(4,128)S(1)} %get-tuple-element.52), channel_id=1, source_target_pairs={{1,0},{2,1},{3,2},{4,3},{5,4},{6,5},{7,6},{8,7},{9,8},{10,9},{11,1... | collective-permute-start | bytes 1640 | tf_op jit(solution)/shard_map/ppermute | solution.py:21
  423.2 12.3 %collective-permute-start.59 = (f32[4,34,1]{2,0,1:T(4,128)S(1)}, f32[4,34,1]{2,0,1:T(4,128)S(1)}, u32[]{:S(2)}, u32[]{:S(2)}) collective-permute-start(f32[4,34,1]{2,0,1:T(4,128)S(1)} %get-tuple-element.53), channel_id=1, source_target_pairs={{0,1},{1,2},{2,3},{3,4},{4,5},{5,6},{6,7},{7,8},{8,9},{9,10},{10,1... | collective-permute-start | bytes 1640 | tf_op jit(solution)/shard_map/ppermute | solution.py:18
  425.6 13.8 %collective-permute-start.94 = (f32[1,256]{1,0:T(1,128)S(1)}, f32[1,256]{1,0:T(1,128)S(1)}, u32[]{:S(2)}, u32[]{:S(2)}) collective-permute-start(f32[1,256]{1,0:T(1,128)S(1)} %get-tuple-element.159), channel_id=1, source_target_pairs={{0,16},{16,32},{32,48},{48,64},{64,80},{80,96},{96,112},{1,17},{17... | collective-permute-start | bytes 3080 | tf_op jit(solution)/shard_map/ppermute | solution.py:18
  445.1 17.6 %collective-permute-start.62 = (f32[4,1,256]{2,0,1:T(4,128)S(1)}, f32[4,1,256]{2,0,1:T(4,128)S(1)}, u32[]{:S(2)}, u32[]{:S(2)}) collective-permute-start(f32[4,1,256]{2,0,1:T(4,128)S(1)} %get-tuple-element.82), channel_id=1, source_target_pairs={{0,16},{16,32},{32,48},{48,64},{64,80},{80,96},{96,112},{1,17},{17... | collective-permute-start | bytes 12296 | tf_op jit(solution)/shard_map/ppermute | solution.py:18
  453.9 11.5 %collective-permute-start.63 = (f32[4,1,256]{2,0,1:T(4,128)S(1)}, f32[4,1,256]{2,0,1:T(4,128)S(1)}, u32[]{:S(2)}, u32[]{:S(2)}) collective-permute-start(f32[4,1,256]{2,0,1:T(4,128)S(1)} %get-tuple-element.83), channel_id=1, source_target_pairs={{16,0},{32,16},{48,32},{64,48},{80,64},{96,80},{112,96},{17,1},{33... | collective-permute-start | bytes 12296 | tf_op jit(solution)/shard_map/ppermute | solution.py:21
  455.9 14.1 %collective-permute-start.96 = (f32[34,1]{1,0:T(8,128)S(1)}, f32[34,1]{1,0:T(8,128)S(1)}, u32[]{:S(2)}, u32[]{:S(2)}) collective-permute-start(f32[34,1]{1,0:T(8,128)S(1)} %get-tuple-element.150), channel_id=1, source_target_pairs={{0,1},{1,2},{2,3},{3,4},{4,5},{5,6},{6,7},{7,8},{8,9},{9,10},{10,1... | collective-permute-start | bytes 416 | tf_op jit(solution)/shard_map/ppermute | solution.py:18
  457.8 12.1 %collective-permute-start.97 = (f32[34,1]{1,0:T(8,128)S(1)}, f32[34,1]{1,0:T(8,128)S(1)}, u32[]{:S(2)}, u32[]{:S(2)}) collective-permute-start(f32[34,1]{1,0:T(8,128)S(1)} %get-tuple-element.149), channel_id=1, source_target_pairs={{1,0},{2,1},{3,2},{4,3},{5,4},{6,5},{7,6},{8,7},{9,8},{10,9},{11,1... | collective-permute-start | bytes 416 | tf_op jit(solution)/shard_map/ppermute | solution.py:21
  475.1 19.4 %collective-permute-start.70 = (f32[1,32,256]{2,0,1:T(1,128)S(1)}, f32[1,32,256]{2,0,1:T(1,128)S(1)}, u32[]{:S(2)}, u32[]{:S(2)}) collective-permute-start(f32[1,32,256]{2,0,1:T(1,128)S(1)} %get-tuple-element.126), channel_id=1, source_target_pairs={{0,128},{128,256},{256,384},{1,129},{129,257},{257,385},{2,130},{1... | collective-permute-start | bytes 98312 | tf_op jit(solution)/shard_map/ppermute | solution.py:18
  478.2 16.2 %collective-permute-start.71 = (f32[1,32,256]{2,0,1:T(1,128)S(1)}, f32[1,32,256]{2,0,1:T(1,128)S(1)}, u32[]{:S(2)}, u32[]{:S(2)}) collective-permute-start(f32[1,32,256]{2,0,1:T(1,128)S(1)} %get-tuple-element.127), channel_id=1, source_target_pairs={{128,0},{256,128},{384,256},{129,1},{257,129},{385,257},{130,2},{2... | collective-permute-start | bytes 98312 | tf_op jit(solution)/shard_map/ppermute | solution.py:21
  501.6 11.5 %collective-permute-start.73 = (f32[4,1,256]{2,0,1:T(4,128)S(1)}, f32[4,1,256]{2,0,1:T(4,128)S(1)}, u32[]{:S(2)}, u32[]{:S(2)}) collective-permute-start(f32[4,1,256]{2,0,1:T(4,128)S(1)} %get-tuple-element.81), channel_id=1, source_target_pairs={{16,0},{32,16},{48,32},{64,48},{80,64},{96,80},{112,96},{17,1},{33... | collective-permute-start | bytes 12296 | tf_op jit(solution)/shard_map/ppermute | solution.py:21
  513.3 17.5 %collective-permute-start.74 = (f32[4,34,1]{2,0,1:T(4,128)S(1)}, f32[4,34,1]{2,0,1:T(4,128)S(1)}, u32[]{:S(2)}, u32[]{:S(2)}) collective-permute-start(f32[4,34,1]{2,0,1:T(4,128)S(1)} %get-tuple-element.48), channel_id=1, source_target_pairs={{1,0},{2,1},{3,2},{4,3},{5,4},{6,5},{7,6},{8,7},{9,8},{10,9},{11,1... | collective-permute-start | bytes 1640 | tf_op jit(solution)/shard_map/ppermute | solution.py:21
  515.2 15.6 %collective-permute-start.75 = (f32[4,34,1]{2,0,1:T(4,128)S(1)}, f32[4,34,1]{2,0,1:T(4,128)S(1)}, u32[]{:S(2)}, u32[]{:S(2)}) collective-permute-start(f32[4,34,1]{2,0,1:T(4,128)S(1)} %get-tuple-element.49), channel_id=1, source_target_pairs={{0,1},{1,2},{2,3},{3,4},{4,5},{5,6},{6,7},{7,8},{8,9},{9,10},{10,1... | collective-permute-start | bytes 1640 | tf_op jit(solution)/shard_map/ppermute | solution.py:18
  541.2 11.5 %collective-permute-start.79 = (f32[4,1,256]{2,0,1:T(4,128)S(1)}, f32[4,1,256]{2,0,1:T(4,128)S(1)}, u32[]{:S(2)}, u32[]{:S(2)}) collective-permute-start(f32[4,1,256]{2,0,1:T(4,128)S(1)} %get-tuple-element.79), channel_id=1, source_target_pairs={{16,0},{32,16},{48,32},{64,48},{80,64},{96,80},{112,96},{17,1},{33... | collective-permute-start | bytes 12296 | tf_op jit(solution)/shard_map/ppermute | solution.py:21
  571.2 19.0 %collective-permute-start.84 = (f32[4,1,256]{2,0,1:T(4,128)S(1)}, f32[4,1,256]{2,0,1:T(4,128)S(1)}, u32[]{:S(2)}, u32[]{:S(2)}) collective-permute-start(f32[4,1,256]{2,0,1:T(4,128)S(1)} %get-tuple-element.76), channel_id=1, source_target_pairs={{0,16},{16,32},{32,48},{48,64},{64,80},{80,96},{96,112},{1,17},{17... | collective-permute-start | bytes 12296 | tf_op jit(solution)/shard_map/ppermute | solution.py:18
  573.1 17.1 %collective-permute-start.85 = (f32[4,1,256]{2,0,1:T(4,128)S(1)}, f32[4,1,256]{2,0,1:T(4,128)S(1)}, u32[]{:S(2)}, u32[]{:S(2)}) collective-permute-start(f32[4,1,256]{2,0,1:T(4,128)S(1)} %get-tuple-element.77), channel_id=1, source_target_pairs={{16,0},{32,16},{48,32},{64,48},{80,64},{96,80},{112,96},{17,1},{33... | collective-permute-start | bytes 12296 | tf_op jit(solution)/shard_map/ppermute | solution.py:21
  590.4 14.2 %collective-permute-start.86 = (f32[4,34,1]{2,0,1:T(4,128)S(1)}, f32[4,34,1]{2,0,1:T(4,128)S(1)}, u32[]{:S(2)}, u32[]{:S(2)}) collective-permute-start(f32[4,34,1]{2,0,1:T(4,128)S(1)} %get-tuple-element.44), channel_id=1, source_target_pairs={{1,0},{2,1},{3,2},{4,3},{5,4},{6,5},{7,6},{8,7},{9,8},{10,9},{11,1... | collective-permute-start | bytes 1640 | tf_op jit(solution)/shard_map/ppermute | solution.py:21
  592.3 12.3 %collective-permute-start.87 = (f32[4,34,1]{2,0,1:T(4,128)S(1)}, f32[4,34,1]{2,0,1:T(4,128)S(1)}, u32[]{:S(2)}, u32[]{:S(2)}) collective-permute-start(f32[4,34,1]{2,0,1:T(4,128)S(1)} %get-tuple-element.45), channel_id=1, source_target_pairs={{0,1},{1,2},{2,3},{3,4},{4,5},{5,6},{6,7},{7,8},{8,9},{9,10},{10,1... | collective-permute-start | bytes 1640 | tf_op jit(solution)/shard_map/ppermute | solution.py:18
  594.8 13.8 %collective-permute-start.122 = (f32[1,256]{1,0:T(1,128)S(1)}, f32[1,256]{1,0:T(1,128)S(1)}, u32[]{:S(2)}, u32[]{:S(2)}) collective-permute-start(f32[1,256]{1,0:T(1,128)S(1)} %get-tuple-element.157), channel_id=1, source_target_pairs={{0,16},{16,32},{32,48},{48,64},{64,80},{80,96},{96,112},{1,17},{17... | collective-permute-start | bytes 3080 | tf_op jit(solution)/shard_map/ppermute | solution.py:18
  614.3 17.6 %collective-permute-start.90 = (f32[4,1,256]{2,0,1:T(4,128)S(1)}, f32[4,1,256]{2,0,1:T(4,128)S(1)}, u32[]{:S(2)}, u32[]{:S(2)}) collective-permute-start(f32[4,1,256]{2,0,1:T(4,128)S(1)} %get-tuple-element.74), channel_id=1, source_target_pairs={{0,16},{16,32},{32,48},{48,64},{64,80},{80,96},{96,112},{1,17},{17... | collective-permute-start | bytes 12296 | tf_op jit(solution)/shard_map/ppermute | solution.py:18
  623.0 11.5 %collective-permute-start.91 = (f32[4,1,256]{2,0,1:T(4,128)S(1)}, f32[4,1,256]{2,0,1:T(4,128)S(1)}, u32[]{:S(2)}, u32[]{:S(2)}) collective-permute-start(f32[4,1,256]{2,0,1:T(4,128)S(1)} %get-tuple-element.75), channel_id=1, source_target_pairs={{16,0},{32,16},{48,32},{64,48},{80,64},{96,80},{112,96},{17,1},{33... | collective-permute-start | bytes 12296 | tf_op jit(solution)/shard_map/ppermute | solution.py:21
  625.0 14.1 %collective-permute-start.124 = (f32[34,1]{1,0:T(8,128)S(1)}, f32[34,1]{1,0:T(8,128)S(1)}, u32[]{:S(2)}, u32[]{:S(2)}) collective-permute-start(f32[34,1]{1,0:T(8,128)S(1)} %get-tuple-element.148), channel_id=1, source_target_pairs={{0,1},{1,2},{2,3},{3,4},{4,5},{5,6},{6,7},{7,8},{8,9},{9,10},{10,1... | collective-permute-start | bytes 416 | tf_op jit(solution)/shard_map/ppermute | solution.py:18
  627.0 12.1 %collective-permute-start.125 = (f32[34,1]{1,0:T(8,128)S(1)}, f32[34,1]{1,0:T(8,128)S(1)}, u32[]{:S(2)}, u32[]{:S(2)}) collective-permute-start(f32[34,1]{1,0:T(8,128)S(1)} %get-tuple-element.147), channel_id=1, source_target_pairs={{1,0},{2,1},{3,2},{4,3},{5,4},{6,5},{7,6},{8,7},{9,8},{10,9},{11,1... | collective-permute-start | bytes 416 | tf_op jit(solution)/shard_map/ppermute | solution.py:21
  644.2 19.4 %collective-permute-start.98 = (f32[1,32,256]{2,0,1:T(1,128)S(1)}, f32[1,32,256]{2,0,1:T(1,128)S(1)}, u32[]{:S(2)}, u32[]{:S(2)}) collective-permute-start(f32[1,32,256]{2,0,1:T(1,128)S(1)} %get-tuple-element.117), channel_id=1, source_target_pairs={{0,128},{128,256},{256,384},{1,129},{129,257},{257,385},{2,130},{1... | collective-permute-start | bytes 98312 | tf_op jit(solution)/shard_map/ppermute | solution.py:18
  647.3 16.2 %collective-permute-start.99 = (f32[1,32,256]{2,0,1:T(1,128)S(1)}, f32[1,32,256]{2,0,1:T(1,128)S(1)}, u32[]{:S(2)}, u32[]{:S(2)}) collective-permute-start(f32[1,32,256]{2,0,1:T(1,128)S(1)} %get-tuple-element.118), channel_id=1, source_target_pairs={{128,0},{256,128},{384,256},{129,1},{257,129},{385,257},{130,2},{2... | collective-permute-start | bytes 98312 | tf_op jit(solution)/shard_map/ppermute | solution.py:21
  670.7 11.5 %collective-permute-start.101 = (f32[4,1,256]{2,0,1:T(4,128)S(1)}, f32[4,1,256]{2,0,1:T(4,128)S(1)}, u32[]{:S(2)}, u32[]{:S(2)}) collective-permute-start(f32[4,1,256]{2,0,1:T(4,128)S(1)} %get-tuple-element.73), channel_id=1, source_target_pairs={{16,0},{32,16},{48,32},{64,48},{80,64},{96,80},{112,96},{17,1},{33... | collective-permute-start | bytes 12296 | tf_op jit(solution)/shard_map/ppermute | solution.py:21
  682.4 17.5 %collective-permute-start.102 = (f32[4,34,1]{2,0,1:T(4,128)S(1)}, f32[4,34,1]{2,0,1:T(4,128)S(1)}, u32[]{:S(2)}, u32[]{:S(2)}) collective-permute-start(f32[4,34,1]{2,0,1:T(4,128)S(1)} %get-tuple-element.40), channel_id=1, source_target_pairs={{1,0},{2,1},{3,2},{4,3},{5,4},{6,5},{7,6},{8,7},{9,8},{10,9},{11,1... | collective-permute-start | bytes 1640 | tf_op jit(solution)/shard_map/ppermute | solution.py:21
  684.4 15.6 %collective-permute-start.103 = (f32[4,34,1]{2,0,1:T(4,128)S(1)}, f32[4,34,1]{2,0,1:T(4,128)S(1)}, u32[]{:S(2)}, u32[]{:S(2)}) collective-permute-start(f32[4,34,1]{2,0,1:T(4,128)S(1)} %get-tuple-element.41), channel_id=1, source_target_pairs={{0,1},{1,2},{2,3},{3,4},{4,5},{5,6},{6,7},{7,8},{8,9},{9,10},{10,1... | collective-permute-start | bytes 1640 | tf_op jit(solution)/shard_map/ppermute | solution.py:18
  710.4 11.5 %collective-permute-start.107 = (f32[4,1,256]{2,0,1:T(4,128)S(1)}, f32[4,1,256]{2,0,1:T(4,128)S(1)}, u32[]{:S(2)}, u32[]{:S(2)}) collective-permute-start(f32[4,1,256]{2,0,1:T(4,128)S(1)} %get-tuple-element.71), channel_id=1, source_target_pairs={{16,0},{32,16},{48,32},{64,48},{80,64},{96,80},{112,96},{17,1},{33... | collective-permute-start | bytes 12296 | tf_op jit(solution)/shard_map/ppermute | solution.py:21
  742.3 11.5 %collective-permute-start.113 = (f32[4,1,256]{2,0,1:T(4,128)S(1)}, f32[4,1,256]{2,0,1:T(4,128)S(1)}, u32[]{:S(2)}, u32[]{:S(2)}) collective-permute-start(f32[4,1,256]{2,0,1:T(4,128)S(1)} %get-tuple-element.69), channel_id=1, source_target_pairs={{16,0},{32,16},{48,32},{64,48},{80,64},{96,80},{112,96},{17,1},{33... | collective-permute-start | bytes 12296 | tf_op jit(solution)/shard_map/ppermute | solution.py:21
  774.9 11.5 %collective-permute-start.119 = (f32[4,1,256]{2,0,1:T(4,128)S(1)}, f32[4,1,256]{2,0,1:T(4,128)S(1)}, u32[]{:S(2)}, u32[]{:S(2)}) collective-permute-start(f32[4,1,256]{2,0,1:T(4,128)S(1)} %get-tuple-element.67), channel_id=1, source_target_pairs={{16,0},{32,16},{48,32},{64,48},{80,64},{96,80},{112,96},{17,1},{33... | collective-permute-start | bytes 12296 | tf_op jit(solution)/shard_map/ppermute | solution.py:21
  786.6 17.5 %collective-permute-start.120 = (f32[4,34,1]{2,0,1:T(4,128)S(1)}, f32[4,34,1]{2,0,1:T(4,128)S(1)}, u32[]{:S(2)}, u32[]{:S(2)}) collective-permute-start(f32[4,34,1]{2,0,1:T(4,128)S(1)} %get-tuple-element.34), channel_id=1, source_target_pairs={{1,0},{2,1},{3,2},{4,3},{5,4},{6,5},{7,6},{8,7},{9,8},{10,9},{11,1... | collective-permute-start | bytes 1640 | tf_op jit(solution)/shard_map/ppermute | solution.py:21
  788.5 15.6 %collective-permute-start.121 = (f32[4,34,1]{2,0,1:T(4,128)S(1)}, f32[4,34,1]{2,0,1:T(4,128)S(1)}, u32[]{:S(2)}, u32[]{:S(2)}) collective-permute-start(f32[4,34,1]{2,0,1:T(4,128)S(1)} %get-tuple-element.35), channel_id=1, source_target_pairs={{0,1},{1,2},{2,3},{3,4},{4,5},{5,6},{6,7},{7,8},{8,9},{9,10},{10,1... | collective-permute-start | bytes 1640 | tf_op jit(solution)/shard_map/ppermute | solution.py:18
  (78 other events, 1152.4 us)
